TPU v7x, 32 devices: a whole 2x2x4 slice. The times are simulated.
32 devices in a mesh: dp: 8 (over z, x), expert: 4 (over y, core).
Axes of the slice: x: 2, y: 2, z: 4, core: 2. Of those that a mesh axis runs over, the one named last changes fastest.
Arguments:
- patches: bfloat16 [16384, 768], P(('dp', 'expert')), may hold values from -6 to 6
- time_embed: bfloat16 [64, 768], P(('dp', 'expert')), may hold values from -6 to 6
- ada_weight: bfloat16 [768, 4608], replicated, may hold values from -0.21875 to 0.21875
- ada_bias: float32 [4608], replicated, may hold values from -3 to 3
- qkv_weight: bfloat16 [768, 2304], replicated, may hold values from -0.21875 to 0.21875
- out_weight: bfloat16 [768, 768], replicated, may hold values from -0.875 to 0.875
- up_weight: bfloat16 [768, 3072], replicated, may hold values from -0.21875 to 0.21875
- down_weight: bfloat16 [3072, 768], replicated, may hold values from -0.109375 to 0.109375
- expert_up: bfloat16 [4, 768, 3072], P('expert'), may hold values from -0.21875 to 0.21875
- expert_down: bfloat16 [4, 3072, 768], P('expert'), may hold values from -0.109375 to 0.109375
- routes: int32 [16384, 2], P(('dp', 'expert')), may hold values from 0 to 3, as said below
- gate_weights: float32 [16384, 2], P(('dp', 'expert')), may hold values from 0.2 to 0.8
- cotangent: bfloat16 [16384, 768], P(('dp', 'expert')), may hold values from -21 to 21
Outputs:
- block_out: bfloat16 [16384, 768], P(('dp', 'expert'))
- grad_input: float32 [16384, 768], P(('dp', 'expert'))
- grad_ada: float32 [768, 4608], P('dp')
- grad_ada_bias: float32 [4608], P('dp')
- grad_qkv: float32 [768, 2304], P('dp')
- grad_out_proj: float32 [768, 768], P('dp')
- grad_up: float32 [768, 3072], P('dp')
- grad_down: float32 [3072, 768], P('dp')
- grad_expert_up: float32 [4, 768, 3072], P('expert', 'dp')
- grad_expert_down: float32 [4, 3072, 768], P('expert', 'dp')
- counts: int32 [4], replicated
Inputs may be any that keep to these rules, and one draw needn't show every extreme that they name: `routes`: each patch names two different experts.
All inputs are finite; a program needn't handle non-finite values.
Results may differ from a plain program's by a relative error of at most 0.019.
The roundings to bfloat16 on the way count: a program that leaves them out, or rounds other values in their place, can miss the bound.
Values may be sent and summed in bfloat16 or wider, within the bound.
No kernel may reach another device: no remote copies, remote signals or barrier semaphores. Data moves between devices by JAX's collectives and lax.ppermute only.
A program may use at most 256 MiB of HBM per device.

v0:
```python
import math

import jax
import jax.numpy as jnp
from jax import lax
from jax.sharding import PartitionSpec as P

HEAD_DIM = 64


SQRT_TWO_OVER_PI = math.sqrt(2.0 / math.pi)


def layer_norm(values_in):
    row_mean = jnp.mean(values_in, axis=-1, keepdims=True)
    centered = values_in - row_mean
    row_var = jnp.mean(centered * centered, axis=-1, keepdims=True)
    return centered * lax.rsqrt(row_var + 1e-06)


def modulate(values_in, shift_part, scale_part):
    return layer_norm(values_in) * (1.0 + scale_part[:, None, :]) + shift_part[:, None, :]


def gelu_tanh(values_in):
    return jax.nn.gelu(values_in, approximate=True)


def gelu_slope(values_in):
    squared = values_in * values_in
    tanh_inner = jnp.tanh(SQRT_TWO_OVER_PI * (values_in + 0.044715 * squared * values_in))
    return 0.5 * (1.0 + tanh_inner) + 0.5 * values_in * (
        1.0 - tanh_inner * tanh_inner
    ) * SQRT_TWO_OVER_PI * (1.0 + 3.0 * 0.044715 * squared)


def contract_rows(left_in, right_in):
    return lax.dot_general(
        left_in, right_in, (((0,), (0,)), ((), ())), preferred_element_type=jnp.float32
    )


def project_back(left_in, right_in):
    return lax.dot_general(
        left_in, right_in, (((1,), (1,)), ((), ())), preferred_element_type=jnp.float32
    )


def on_device(
    patches,
    time_embed,
    ada_weight,
    ada_bias,
    qkv_weight,
    out_weight,
    up_weight,
    down_weight,
    expert_up,
    expert_down,
    routes,
    gate_weights,
    cotangent,
):
    tokens, model_width = patches.shape
    latents = time_embed.shape[0]
    seq_len = tokens // latents
    head_count = model_width // HEAD_DIM
    experts = lax.axis_size("expert")
    capacity = 5 * tokens // (2 * experts)
    scale_factor = HEAD_DIM ** (-0.5)
    pair_expert = routes.reshape(tokens * 2)
    expert_hot = (pair_expert[:, None] == jnp.arange(experts, dtype=jnp.int32)[None, :]).astype(
        jnp.int32
    )
    earlier = jnp.cumsum(expert_hot, axis=0) - expert_hot
    slot_index = jnp.sum(earlier * expert_hot, axis=1)
    target = jnp.where(
        slot_index < capacity, pair_expert * capacity + slot_index, experts * capacity
    ).reshape(tokens, 2)
    columns = jnp.arange(experts * capacity, dtype=jnp.int32)
    pick_first = (target[:, 0:1] == columns[None, :]).astype(jnp.bfloat16)
    pick_second = (target[:, 1:2] == columns[None, :]).astype(jnp.bfloat16)
    pick_both = pick_first + pick_second
    local_counts = jnp.sum(expert_hot, axis=0)
    cond_act = jax.nn.silu(time_embed.astype(jnp.float32)).astype(jnp.bfloat16)
    modulation = jnp.dot(cond_act, ada_weight, preferred_element_type=jnp.float32) + ada_bias
    shift_one, scale_one, gate_one, shift_two, scale_two, gate_two = jnp.split(
        modulation, 6, axis=1
    )
    residual_in = patches.astype(jnp.float32).reshape(latents, seq_len, model_width)
    first_full, first_pull = jax.vjp(modulate, residual_in, shift_one, scale_one)
    first_in = first_full.reshape(tokens, model_width).astype(jnp.bfloat16)
    qkv_all = jnp.dot(first_in, qkv_weight, preferred_element_type=jnp.float32).astype(jnp.bfloat16)
    head_shape = (latents, seq_len, head_count, HEAD_DIM)
    queries = qkv_all[:, :model_width].reshape(head_shape)
    keys_all = qkv_all[:, model_width : 2 * model_width].reshape(head_shape)
    values_all = qkv_all[:, 2 * model_width :].reshape(head_shape)
    scores = (
        jnp.einsum("bqhd,bkhd->bhqk", queries, keys_all, preferred_element_type=jnp.float32)
        * scale_factor
    )
    row_peak = jnp.max(scores, axis=-1, keepdims=True)
    shifted_exp = jnp.exp(scores - row_peak)
    row_total = jnp.sum(shifted_exp, axis=-1, keepdims=True)
    log_total = row_peak + jnp.log(row_total)
    probs_low = (shifted_exp / row_total).astype(jnp.bfloat16)
    attended = jnp.einsum(
        "bhqk,bkhd->bqhd", probs_low, values_all, preferred_element_type=jnp.float32
    )
    attended = attended.reshape(tokens, model_width).astype(jnp.bfloat16)
    attn_proj = jnp.dot(attended, out_weight, preferred_element_type=jnp.float32).reshape(
        latents, seq_len, model_width
    )
    middle = residual_in + gate_one[:, None, :] * attn_proj
    second_full, second_pull = jax.vjp(modulate, middle, shift_two, scale_two)
    second_in = second_full.reshape(tokens, model_width).astype(jnp.bfloat16)
    shared_pre = jnp.dot(second_in, up_weight, preferred_element_type=jnp.float32)
    shared_act = gelu_tanh(shared_pre).astype(jnp.bfloat16)
    shared_out = jnp.dot(shared_act, down_weight, preferred_element_type=jnp.float32)
    dispatched = (
        contract_rows(pick_both, second_in)
        .astype(jnp.bfloat16)
        .reshape(experts, capacity, model_width)
    )
    up_matrix = expert_up[0]
    down_matrix = expert_down[0]
    arrived = lax.all_to_all(dispatched, "expert", split_axis=0, concat_axis=0, tiled=True)
    rows_in = arrived.reshape(-1, model_width)
    pre_act = jnp.dot(rows_in, up_matrix, preferred_element_type=jnp.float32)
    act_rows = gelu_tanh(pre_act).astype(jnp.bfloat16)
    out_rows = jnp.dot(act_rows, down_matrix, preferred_element_type=jnp.float32).astype(
        jnp.bfloat16
    )
    item_shape = (arrived.shape[0], arrived.shape[1], -1)
    expert_out = out_rows.reshape(item_shape)
    expert_pre = pre_act.reshape(item_shape)
    expert_act = act_rows.reshape(item_shape)
    returned = lax.all_to_all(
        expert_out, "expert", split_axis=0, concat_axis=0, tiled=True
    ).reshape(experts * capacity, model_width)
    first_sel = jnp.dot(pick_first, returned, preferred_element_type=jnp.float32)
    second_sel = jnp.dot(pick_second, returned, preferred_element_type=jnp.float32)
    mixture = gate_weights[:, 0:1] * first_sel + gate_weights[:, 1:2] * second_sel
    branch = (shared_out + mixture).reshape(latents, seq_len, model_width)
    result = middle + gate_two[:, None, :] * branch
    block_out = result.reshape(tokens, model_width).astype(jnp.bfloat16)
    grad_result = cotangent.astype(jnp.float32).reshape(latents, seq_len, model_width)
    grad_gate_two = jnp.sum(grad_result * branch, axis=1)
    grad_branch = (gate_two[:, None, :] * grad_result).reshape(tokens, model_width)
    grad_shared = grad_branch.astype(jnp.bfloat16)
    grad_first_pair = (gate_weights[:, 0:1] * grad_branch).astype(jnp.bfloat16)
    grad_second_pair = (gate_weights[:, 1:2] * grad_branch).astype(jnp.bfloat16)
    grad_slots = contract_rows(pick_first, grad_first_pair) + contract_rows(
        pick_second, grad_second_pair
    )
    grad_slots = grad_slots.astype(jnp.bfloat16).reshape(experts, capacity, model_width)
    grad_arrived = lax.all_to_all(grad_slots, "expert", split_axis=0, concat_axis=0, tiled=True)
    grad_rows_out = grad_arrived.reshape(-1, model_width)
    pre_flat = expert_pre.reshape(-1, expert_pre.shape[2])
    act_flat = expert_act.reshape(-1, expert_act.shape[2])
    rows_flat = arrived.reshape(-1, model_width)
    grad_e_down = contract_rows(act_flat, grad_rows_out)
    grad_e_act = project_back(grad_rows_out, down_matrix)
    grad_e_pre = (grad_e_act * gelu_slope(pre_flat)).astype(jnp.bfloat16)
    grad_e_up = contract_rows(rows_flat, grad_e_pre)
    grad_rows_in = project_back(grad_e_pre, up_matrix).astype(jnp.bfloat16).reshape(arrived.shape)
    grad_back = lax.all_to_all(
        grad_rows_in, "expert", split_axis=0, concat_axis=0, tiled=True
    ).reshape(experts * capacity, model_width)
    grad_w_down = contract_rows(shared_act, grad_shared)
    grad_shared_act = project_back(grad_shared, down_weight)
    grad_shared_pre = (grad_shared_act * gelu_slope(shared_pre)).astype(jnp.bfloat16)
    grad_w_up = contract_rows(second_in, grad_shared_pre)
    grad_second = project_back(grad_shared_pre, up_weight) + jnp.dot(
        pick_both, grad_back, preferred_element_type=jnp.float32
    )
    grad_mid_norm, grad_shift_two, grad_scale_two = second_pull(
        grad_second.reshape(latents, seq_len, model_width)
    )
    grad_middle = grad_result + grad_mid_norm
    grad_gate_one = jnp.sum(grad_middle * attn_proj, axis=1)
    grad_attn = (
        (gate_one[:, None, :] * grad_middle).reshape(tokens, model_width).astype(jnp.bfloat16)
    )
    grad_w_out = contract_rows(attended, grad_attn)
    grad_attended = project_back(grad_attn, out_weight).astype(jnp.bfloat16).reshape(head_shape)
    scores_again = (
        jnp.einsum("bqhd,bkhd->bhqk", queries, keys_all, preferred_element_type=jnp.float32)
        * scale_factor
    )
    attn_probs = jnp.exp(scores_again - log_total)
    probs_again = attn_probs.astype(jnp.bfloat16)
    grad_values = jnp.einsum(
        "bhqk,bqhd->bkhd", probs_again, grad_attended, preferred_element_type=jnp.float32
    )
    grad_probs = jnp.einsum(
        "bqhd,bkhd->bhqk", grad_attended, values_all, preferred_element_type=jnp.float32
    )
    grad_scores = (
        attn_probs * (grad_probs - jnp.sum(attn_probs * grad_probs, axis=-1, keepdims=True))
    ).astype(jnp.bfloat16)
    grad_queries = (
        jnp.einsum("bhqk,bkhd->bqhd", grad_scores, keys_all, preferred_element_type=jnp.float32)
        * scale_factor
    )
    grad_keys = (
        jnp.einsum("bhqk,bqhd->bkhd", grad_scores, queries, preferred_element_type=jnp.float32)
        * scale_factor
    )
    grad_qkv_rows = jnp.concatenate(
        [
            grad_queries.reshape(tokens, model_width),
            grad_keys.reshape(tokens, model_width),
            grad_values.reshape(tokens, model_width),
        ],
        axis=1,
    ).astype(jnp.bfloat16)
    grad_w_qkv = contract_rows(first_in, grad_qkv_rows)
    grad_first = project_back(grad_qkv_rows, qkv_weight)
    grad_in_norm, grad_shift_one, grad_scale_one = first_pull(
        grad_first.reshape(latents, seq_len, model_width)
    )
    grad_input = (grad_middle + grad_in_norm).reshape(tokens, model_width)
    grad_modulation = jnp.concatenate(
        [
            grad_shift_one,
            grad_scale_one,
            grad_gate_one,
            grad_shift_two,
            grad_scale_two,
            grad_gate_two,
        ],
        axis=1,
    )
    grad_w_ada = lax.dot_general(
        cond_act.astype(jnp.float32),
        grad_modulation,
        (((0,), (0,)), ((), ())),
        precision=lax.Precision.HIGHEST,
    )
    grad_b_ada = jnp.sum(grad_modulation, axis=0)
    dense_shares = (
        lax.psum_scatter(
            grad_w_ada.astype(jnp.bfloat16), "dp", scatter_dimension=0, tiled=True
        ).astype(jnp.float32),
        lax.psum_scatter(
            grad_b_ada.astype(jnp.bfloat16), "dp", scatter_dimension=0, tiled=True
        ).astype(jnp.float32),
        lax.psum_scatter(
            grad_w_qkv.astype(jnp.bfloat16), "dp", scatter_dimension=0, tiled=True
        ).astype(jnp.float32),
        lax.psum_scatter(
            grad_w_out.astype(jnp.bfloat16), "dp", scatter_dimension=0, tiled=True
        ).astype(jnp.float32),
        lax.psum_scatter(
            grad_w_up.astype(jnp.bfloat16), "dp", scatter_dimension=0, tiled=True
        ).astype(jnp.float32),
        lax.psum_scatter(
            grad_w_down.astype(jnp.bfloat16), "dp", scatter_dimension=0, tiled=True
        ).astype(jnp.float32),
    )
    summed = (
        lax.psum(dense_shares[0].astype(jnp.bfloat16), "expert").astype(jnp.float32),
        lax.psum(dense_shares[1].astype(jnp.bfloat16), "expert").astype(jnp.float32),
        lax.psum(dense_shares[2].astype(jnp.bfloat16), "expert").astype(jnp.float32),
        lax.psum(dense_shares[3].astype(jnp.bfloat16), "expert").astype(jnp.float32),
        lax.psum(dense_shares[4].astype(jnp.bfloat16), "expert").astype(jnp.float32),
        lax.psum(dense_shares[5].astype(jnp.bfloat16), "expert").astype(jnp.float32),
    )
    expert_sums = (
        lax.psum_scatter(
            grad_e_up[None].astype(jnp.bfloat16), "dp", scatter_dimension=1, tiled=True
        ).astype(jnp.float32),
        lax.psum_scatter(
            grad_e_down[None].astype(jnp.bfloat16), "dp", scatter_dimension=1, tiled=True
        ).astype(jnp.float32),
    )
    counts = lax.psum(local_counts, ("dp", "expert"))
    return (
        block_out,
        grad_input,
        summed[0],
        summed[1],
        summed[2],
        summed[3],
        summed[4],
        summed[5],
        expert_sums[0],
        expert_sums[1],
        counts,
    )


def solution(mesh):
    in_specs = (
        P(("dp", "expert"), None),
        P(("dp", "expert"), None),
        P(),
        P(),
        P(),
        P(),
        P(),
        P(),
        P("expert", None, None),
        P("expert", None, None),
        P(("dp", "expert"), None),
        P(("dp", "expert"), None),
        P(("dp", "expert"), None),
    )
    out_specs = (
        P(("dp", "expert"), None),
        P(("dp", "expert"), None),
        P("dp", None),
        P("dp"),
        P("dp", None),
        P("dp", None),
        P("dp", None),
        P("dp", None),
        P("expert", "dp", None),
        P("expert", "dp", None),
        P(),
    )
    return jax.shard_map(
        on_device, mesh=mesh, in_specs=in_specs, out_specs=out_specs, check_vma=False
    )
```

profile of v0, /device:TPU:0, one launch (start us, length us, event | category | flops | bytes accessed | tf_op | source)
XLA Modules:
  0.0 971.1 jit_solution(989283196420073789)
XLA Ops:
  74.0 4.7 all-to-all-start
  81.5 4.6 fusion.121
  89.3 6.4 fusion.27
  95.7 8.0 all-to-all-done
  103.7 4.9 all-to-all-start.2
  108.6 8.8 fusion.36
  117.4 5.5 copy-done.63
  122.9 12.6 %fusion.44 = bf16[1280,768]{1,0:T(8,128)(2,1)} fusion(bf16[1,3072,768]{2,1,0:T(8,128)(2,1)} %param.22, f32[1280,3072]{1,0:T(8,128)S(1)} %fusion.36), kind=kOutput, calls=%fused_computation.65 | convolution fusion | flops 6076170240 | bytes 22413312 | tf_op jit(solution)/shard_map/dot_general | solution.py:131
  135.4 4.6 all-to-all-start.1
  140.0 17.7 %fusion.12 = bf16[1280,3072]{1,0:T(8,128)(2,1)S(1)} fusion(f32[1280,3072]{1,0:T(8,128)} %copy-done.63, bf16[1280,768]{1,0:T(8,128)(2,1)} %bitcast.21, bf16[1,3072,768]{2,1,0:T(8,128)(2,1)} %param.22), kind=kOutput, calls=%fused_computation.16 | convolution fusion | flops 6110576640 | bytes 30277632 | tf_op jit(solution)/shard_map/dot_general | solution.py:44
  160.8 9.8 %fusion.41 = bf16[1280,768]{1,0:T(8,128)(2,1)} fusion(bf16[1280,3072]{1,0:T(8,128)(2,1)S(1)} %fusion.12, bf16[1,768,3072]{2,1,0:T(8,128)(2,1)} %param.21), kind=kOutput, calls=%fused_computation.64 | convolution fusion | flops 6040780800 | bytes 14548992 | tf_op jit(solution)/shard_map/dot_general | solution.py:44
  175.4 7.1 fusion.122
  184.4 9.0 fusion.112
  216.6 8.4 convolution_convert_fusion.3
  225.0 6.9 convolution_convert_fusion.4
  247.7 7.3 multiply_reduce_fusion
  255.0 4.6 multiply_convert_fusion
  270.6 5.7 multiply_reduce_fusion.4
  281.4 4.6 fusion.64
  286.8 7.9 convolution_convert_fusion
  294.7 13.7 %fusion.39 = bf16[1,3072,768]{2,1,0:T(8,128)(2,1)} fusion(bf16[1280,768]{1,0:T(8,128)(2,1)} %bitcast.21, f32[1280,3072]{1,0:T(8,128)} %copy-done.63), kind=kOutput, calls=%fused_computation.60 | convolution fusion | flops 6077546496 | bytes 22413312 | tf_op jit(solution)/shard_map/dot_general | solution.py:38
  308.8 10.9 %fusion.38 = bf16[1,768,3072]{2,1,0:T(8,128)(2,1)} fusion(bf16[1280,768]{1,0:T(8,128)(2,1)} %bitcast.10, bf16[1280,3072]{1,0:T(8,128)(2,1)} %copy-done.62), kind=kOutput, calls=%fused_computation.59 | convolution fusion | flops 6042157056 | bytes 14548992 | tf_op jit(solution)/shard_map/dot_general | solution.py:38
  319.8 60.0 %reduce-scatter.16.cloned.1.call-done = bf16[384,768]{1,0:T(8,128)(2,1)} async-done(((bf16[3072,768]{1,0:T(8,128)(2,1)}), bf16[384,768]{1,0:T(8,128)(2,1)}) %reduce-scatter.16.cloned.1.call-update) | async-done | bytes 589840 | tf_op jit(solution)/shard_map/reduce_scatter | solution.py:258
  379.7 98.7 %reduce-scatter.14.cloned.1.call-done = bf16[96,3072]{1,0:T(8,128)(2,1)} async-done(((bf16[768,3072]{1,0:T(8,128)(2,1)}), bf16[96,3072]{1,0:T(8,128)(2,1)}) %reduce-scatter.14.cloned.1.call-update) | async-done | bytes 589840 | tf_op jit(solution)/shard_map/reduce_scatter | solution.py:255
  478.4 82.5 %reduce-scatter.10.cloned.1.call-done = bf16[96,2304]{1,0:T(8,128)(2,1)} async-done(((bf16[768,2304]{1,0:T(8,128)(2,1)}), bf16[96,2304]{1,0:T(8,128)(2,1)}) %reduce-scatter.10.cloned.1.call-update) | async-done | bytes 442384 | tf_op jit(solution)/shard_map/reduce_scatter | solution.py:249
  560.9 132.1 %reduce-scatter.8.cloned.1.call-done = bf16[96,4608]{1,0:T(8,128)(2,1)} async-done(((bf16[768,4608]{1,0:T(8,128)(2,1)}), bf16[96,4608]{1,0:T(8,128)(2,1)}) %reduce-scatter.8.cloned.1.call-update) | async-done | bytes 884752 | tf_op jit(solution)/shard_map/reduce_scatter | solution.py:243
  693.0 41.7 %psum.55 = s32[4]{0:T(128)} all-reduce(s32[4]{0:T(128)S(1)} %copy-done.58), channel_id=1, replica_groups=mesh['dp'=8,'expert'=4] {'dp','expert'}, use_global_device_ids=true, to_apply=%region_36.37 | all-reduce | flops 4 | bytes 32 | tf_op jit(solution)/shard_map/psum | solution.py:278
  736.8 37.1 %all-reduce = bf16[4608]{0:T(1024)(128)(2,1)} all-reduce(bf16[4608]{0:T(1024)(128)(2,1)S(1)} %reduce_sum.226), channel_id=3, replica_groups=mesh['dp'=8,'expert'=4] {'dp'}, use_global_device_ids=true, to_apply=%region_23.24.clone | all-reduce | flops 4608 | bytes 18432
  774.6 6.0 psum.50
  781.3 11.9 %reduce-scatter.20.cloned.1.call-done = bf16[1,384,768]{2,1,0:T(8,128)(2,1)} async-done(((bf16[1,3072,768]{2,1,0:T(8,128)(2,1)}), bf16[1,384,768]{2,1,0:T(8,128)(2,1)}) %reduce-scatter.20.cloned.1.call-update) | async-done | bytes 589840 | tf_op jit(solution)/shard_map/reduce_scatter | solution.py:274
  795.3 97.1 %reduce-scatter.18.cloned.1.call-done = bf16[1,96,3072]{2,1,0:T(8,128)(2,1)} async-done(((bf16[1,768,3072]{2,1,0:T(8,128)(2,1)}), bf16[1,96,3072]{2,1,0:T(8,128)(2,1)}) %reduce-scatter.18.cloned.1.call-update) | async-done | bytes 589840 | tf_op jit(solution)/shard_map/reduce_scatter | solution.py:271
  894.6 61.7 %all-reduce.4.cloned.1.call-done = (bf16[96,4608]{1,0:T(8,128)(2,1)}, bf16[96,2304]{1,0:T(8,128)(2,1)}, bf16[96,768]{1,0:T(8,128)(2,1)}, bf16[96,3072]{1,0:T(8,128)(2,1)}, bf16[384,768]{1,0:T(8,128)(2,1)}) async-done(((bf16[96,4608]{1,0:T(8,128)(2,1)}, bf16[96,2304]{1,0:T(8,128)(2,1)}, bf16[96,768]{1,0:T(8,128)(2,1)}, bf16[96,3072]{1,0:T(8,128)(2,1)}, bf16[384,768]{1,0:T(8,128)(2,1)}), ...) | async-done | bytes 2654224 | tf_op jit(solution)/shard_map/psum | solution.py:263
  (253 shorter events, 152.6 us)
Async XLA Ops:
  7.2 34.1 %copy-start = (bf16[768,2304]{1,0:T(8,128)(2,1)S(1)}, bf16[768,2304]{1,0:T(8,128)(2,1)}, u32[]{:S(2)}) copy-start(bf16[768,2304]{1,0:T(8,128)(2,1)} %param.17) | copy-start | bytes 10616836
  23.0 18.2 %copy-start.32 = (f32[2,768]{1,0:T(2,128)}, f32[2,768]{1,0:T(2,128)S(1)}, u32[]{:S(2)}) copy-start(f32[2,768]{1,0:T(2,128)S(1)} %get-tuple-element.41) | copy-start | bytes 18436
  74.0 29.7 %all-to-all-start = ((bf16[4,320,768]{2,1,0:T(8,128)(2,1)}), bf16[4,320,768]{2,1,0:T(8,128)(2,1)}, u32[]{:S(2)}, u32[]{:S(2)}) async-start(bf16[4,320,768]{2,1,0:T(8,128)(2,1)} %bitcast.186), calls=%async_computation | async-start | bytes 3932160 | tf_op jit(solution)/shard_map/all_to_all | solution.py:127
  78.7 10.5 %slice-start.2 = ((s8[4718592]{0:T(1024)(128)(4,1)}), s8[4194304]{0:T(1024)(128)(4,1)S(1)}, s32[]{:S(2)}) async-start(s8[4718592]{0:T(1024)(128)(4,1)} %bitcast.198), calls=%async_computation.21 | async-start | bytes 8388608
  81.4 7.8 slice-start.3
  103.7 31.7 %all-to-all-start.2 = ((bf16[4,320,768]{2,1,0:T(8,128)(2,1)}), bf16[4,320,768]{2,1,0:T(8,128)(2,1)}, u32[]{:S(2)}, u32[]{:S(2)}) async-start(bf16[4,320,768]{2,1,0:T(8,128)(2,1)} %bitcast.185), calls=%async_computation.2 | async-start | bytes 3932160 | tf_op jit(solution)/shard_map/all_to_all | solution.py:157
  117.4 5.5 copy-start.63
  135.4 35.3 %all-to-all-start.1 = ((bf16[4,320,768]{2,1,0:T(8,128)(2,1)}), bf16[4,320,768]{2,1,0:T(8,128)(2,1)}, u32[]{:S(2)}, u32[]{:S(2)}) async-start(bf16[4,320,768]{2,1,0:T(8,128)(2,1)} %bitcast.187), calls=%async_computation.1 | async-start | bytes 3932160 | tf_op jit(solution)/shard_map/all_to_all | solution.py:138
  170.7 28.8 %all-to-all-start.3 = ((bf16[4,320,768]{2,1,0:T(8,128)(2,1)}), bf16[4,320,768]{2,1,0:T(8,128)(2,1)}, u32[]{:S(2)}, u32[]{:S(2)}) async-start(bf16[4,320,768]{2,1,0:T(8,128)(2,1)} %bitcast.184), calls=%async_computation.3 | async-start | bytes 3932160 | tf_op jit(solution)/shard_map/all_to_all | solution.py:167
  175.1 144.6 %reduce-scatter.12.cloned.1.call-start = ((), (), s32[]{:S(2)}) async-start(), calls=%async_computation.13 | async-start | bytes 1327104 | tf_op jit(solution)/shard_map/reduce_scatter | solution.py:252
  175.4 7.2 copy-start.18
  184.4 9.0 copy-start.57
  209.9 4.9 copy-start.20
  216.6 163.2 %reduce-scatter.16.cloned.1.call-start = ((), (), s32[]{:S(2)}) async-start(), calls=%async_computation.15 | async-start | bytes 5308416 | tf_op jit(solution)/shard_map/reduce_scatter | solution.py:258
  225.0 253.4 %reduce-scatter.14.cloned.1.call-start = ((), (), s32[]{:S(2)}) async-start(), calls=%async_computation.14 | async-start | bytes 5308416 | tf_op jit(solution)/shard_map/reduce_scatter | solution.py:255
  232.0 328.9 %reduce-scatter.10.cloned.1.call-start = ((), (), s32[]{:S(2)}) async-start(), calls=%async_computation.12 | async-start | bytes 3981312 | tf_op jit(solution)/shard_map/reduce_scatter | solution.py:249
  247.1 7.8 slice-start
  247.7 7.3 slice-start.1
  268.8 424.2 %reduce-scatter.8.cloned.1.call-start = ((), (), s32[]{:S(2)}) async-start(), calls=%async_computation.11 | async-start | bytes 7962624 | tf_op jit(solution)/shard_map/reduce_scatter | solution.py:243
  270.6 7.0 copy-start.45
  281.4 4.7 copy-start.43
  281.4 4.7 copy-start.42
  281.4 4.7 copy-start.41
  281.4 4.7 copy-start.52
  281.4 5.3 copy-start.48
  294.7 498.5 %reduce-scatter.20.cloned.1.call-start = ((), (), s32[]{:S(2)}) async-start(), calls=%async_computation.17 | async-start | bytes 5308416 | tf_op jit(solution)/shard_map/reduce_scatter | solution.py:274
  308.5 584.0 %reduce-scatter.18.cloned.1.call-start = ((), (), s32[]{:S(2)}) async-start(), calls=%async_computation.16 | async-start | bytes 5308416 | tf_op jit(solution)/shard_map/reduce_scatter | solution.py:271
  319.7 373.4 %copy-start.58 = (s32[4]{0:T(128)S(1)}, s32[4]{0:T(128)}, u32[]{:S(2)}) copy-start(s32[4]{0:T(128)} %get-tuple-element.18) | copy-start | bytes 52
  319.7 415.1 %copy-start.59 = (u32[32]{0:T(128)S(1)}, u32[32]{0:T(128)}, u32[]{:S(2)}) copy-start(u32[32]{0:T(128)} %constant.54) | copy-start | bytes 388
  319.7 636.6 %all-reduce.4.cloned.1.call-start = ((), (), s32[]{:S(2)}) async-start(), calls=%async_computation.18 | async-start | bytes 5308416 | tf_op jit(solution)/shard_map/psum | solution.py:263
  956.3 5.3 copy-start.27
  956.3 6.4 copy-start.26
  (48 other events, 107.0 us)
Sparse Core Ops, SparseCore 0:
  216.7 65.0 reduce-scatter.11
  285.5 94.2 reduce-scatter.15
  383.4 94.9 reduce-scatter.13
  481.9 78.9 reduce-scatter.9
  564.4 128.5 reduce-scatter.7
  696.9 96.1 reduce-scatter.19
  797.3 95.1 reduce-scatter.17
  895.3 60.9 all-reduce.3
where the time goes:
time: 980 us; the launch traced here: 971 us
  waiting for transfers between devices  554 us (57%)
  matrix products  184 us (19%)
  blocking collectives  84.8 us (9%)
  local copies, waits for them, and re-layouts  60.4 us (6%)
  other arithmetic  52 us (5%)
  starting transfers between devices  19.6 us (2%)
  between operations  16.1 us (2%)
    reduce_scatter x1, waiting for transfers between devices, on_device(): lax.psum_scatter(grad_w_ada.astype(jnp.bfloat16), 'dp', scatter_dimension...  132 us
    reduce_scatter x1, waiting for transfers between devices, on_device(): lax.psum_scatter(grad_w_up.astype(jnp.bfloat16), 'dp', scatter_dimension=...  98.7 us
    reduce_scatter x1, waiting for transfers between devices, on_device(): lax.psum_scatter(grad_e_up[None].astype(jnp.bfloat16), 'dp', scatter_dime...  97.1 us
    reduce_scatter x1, waiting for transfers between devices, on_device(): lax.psum_scatter(grad_w_qkv.astype(jnp.bfloat16), 'dp', scatter_dimension...  82.5 us
    psum x1, waiting for transfers between devices, on_device(): lax.psum(dense_shares[0].astype(jnp.bfloat16), 'expert').astype(jnp.float32)  61.7 us
    reduce_scatter x1, waiting for transfers between devices, on_device(): lax.psum_scatter(grad_w_down.astype(jnp.bfloat16), 'dp', scatter_dimensio...  60 us
    dot_general x9, matrix products, contract_rows(): lax.dot_general(left_in, right_in, (((0,), (0,)), ((), ())), preferred_el...  54.2 us
    dot_general x6, matrix products, project_back(): lax.dot_general(left_in, right_in, (((1,), (1,)), ((), ())), preferred_el...  50 us
  transfers between devices with their start and end apart: 12, of which 9 were waited for; matrix products, arithmetic and copies ran while one was open for 20% of the time, Pallas kernels for 0%

commit v1 on v0

v1 whole, which is shorter than its diff:
```python
import math

import jax
import jax.numpy as jnp
from jax import lax
from jax.sharding import PartitionSpec as P

HEAD_DIM = 64


SQRT_TWO_OVER_PI = math.sqrt(2.0 / math.pi)


def layer_norm(values_in):
    row_mean = jnp.mean(values_in, axis=-1, keepdims=True)
    centered = values_in - row_mean
    row_var = jnp.mean(centered * centered, axis=-1, keepdims=True)
    return centered * lax.rsqrt(row_var + 1e-06)


def modulate(values_in, shift_part, scale_part):
    return layer_norm(values_in) * (1.0 + scale_part[:, None, :]) + shift_part[:, None, :]


def gelu_tanh(values_in):
    return jax.nn.gelu(values_in, approximate=True)


def gelu_slope(values_in):
    squared = values_in * values_in
    tanh_inner = jnp.tanh(SQRT_TWO_OVER_PI * (values_in + 0.044715 * squared * values_in))
    return 0.5 * (1.0 + tanh_inner) + 0.5 * values_in * (
        1.0 - tanh_inner * tanh_inner
    ) * SQRT_TWO_OVER_PI * (1.0 + 3.0 * 0.044715 * squared)


def contract_rows(left_in, right_in):
    return lax.dot_general(
        left_in, right_in, (((0,), (0,)), ((), ())), preferred_element_type=jnp.float32
    )


def project_back(left_in, right_in):
    return lax.dot_general(
        left_in, right_in, (((1,), (1,)), ((), ())), preferred_element_type=jnp.float32
    )


def bits_of(size):
    return size.bit_length() - 1


def label_of(index):
    upper = index >> 1
    return ((upper ^ (upper >> 1)) << 1) | (index & 1)


def index_of(label):
    upper = label >> 1
    shift = 1
    while shift < 32:
        upper = upper ^ (upper >> shift)
        shift *= 2
    return (upper << 1) | (label & 1)


def swap_dp(value, bit):
    size = lax.axis_size("dp")
    return lax.ppermute(
        value, "dp", [(i, index_of(label_of(i) ^ (1 << bit))) for i in range(size)]
    )


def swap_expert(value, bit):
    size = lax.axis_size("expert")
    return lax.ppermute(value, "expert", [(i, i ^ (1 << bit)) for i in range(size)])


def gather_expert(value):
    held = value[None]
    bits = bits_of(lax.axis_size("expert"))
    parts = {0: value}
    for bit in reversed(range(bits)):
        known = list(parts)
        for r in known:
            parts[r | (1 << bit)] = swap_expert(parts[r], bit)
    return jnp.stack([parts[r] for r in range(1 << bits)])


def gather_ordered(value):
    mine = lax.axis_index("expert")
    for bit in range(bits_of(lax.axis_size("expert"))):
        other = swap_expert(value, bit)
        upper = (mine >> bit & 1) == 1
        value = jnp.concatenate(
            [jnp.where(upper, other, value), jnp.where(upper, value, other)], axis=0
        )
    return value


def scatter_expert(parts):
    for bit in range(bits_of(lax.axis_size("expert"))):
        kept = {}
        for r, value in parts.items():
            if r >> bit & 1:
                continue
            other = swap_expert(parts[r | (1 << bit)].astype(jnp.bfloat16), bit)
            kept[r] = value.astype(jnp.float32) + other.astype(jnp.float32)
        parts = kept
    return parts[0]


def gather_dp(value):
    for bit in range(bits_of(lax.axis_size("dp"))):
        value = jnp.concatenate([value, swap_dp(value, bit)], axis=0)
    return value


def scatter_dp(shards, order):
    for bit in order:
        low = [r for r in sorted(shards) if not r >> bit & 1]
        away = jnp.stack([shards[r | (1 << bit)] for r in low])
        came = swap_dp(away, bit)
        shards = {
            r: (shards[r].astype(jnp.float32) + came[i].astype(jnp.float32)).astype(jnp.bfloat16)
            for i, r in enumerate(low)
        }
    return shards[0]


def relative_shards(matrix, size):
    mine = label_of(lax.axis_index("dp"))
    rows = matrix.shape[0] // size
    return {
        r: lax.dynamic_slice_in_dim(matrix, index_of(mine ^ r) * rows, rows, axis=0)
        for r in range(size)
    }


def orders(size):
    bits = bits_of(size)
    return [[(start + step) % bits for step in range(bits)] for start in range(bits)]


def sum_over_dp(matrix, order):
    size = lax.axis_size("dp")
    return scatter_dp(relative_shards(matrix.astype(jnp.bfloat16), size), order)


def sum_over_all(matrix, order):
    core = lax.axis_index("expert") & 1
    half = matrix.shape[1] // 2
    low = matrix.astype(jnp.bfloat16)
    mine = lax.dynamic_slice_in_dim(low, core * half, half, axis=1)
    other = lax.dynamic_slice_in_dim(low, (1 - core) * half, half, axis=1)
    mine = (mine.astype(jnp.float32) + swap_expert(other, 0).astype(jnp.float32)).astype(
        jnp.bfloat16
    )
    total = sum_over_dp(mine, order)
    for bit in range(1, bits_of(lax.axis_size("expert"))):
        total = (
            total.astype(jnp.float32) + swap_expert(total, bit).astype(jnp.float32)
        ).astype(jnp.bfloat16)
    opposite = swap_expert(total, 0)
    first = jnp.where(core == 0, total, opposite)
    second = jnp.where(core == 0, opposite, total)
    return jnp.concatenate([first, second], axis=1).astype(jnp.float32)


def on_device(
    patches,
    time_embed,
    ada_weight,
    ada_bias,
    qkv_weight,
    out_weight,
    up_weight,
    down_weight,
    expert_up,
    expert_down,
    routes,
    gate_weights,
    cotangent,
):
    tokens, model_width = patches.shape
    latents = time_embed.shape[0]
    seq_len = tokens // latents
    head_count = model_width // HEAD_DIM
    experts = lax.axis_size("expert")
    dp_size = lax.axis_size("dp")
    dp_index = lax.axis_index("dp")
    expert_index = lax.axis_index("expert")
    capacity = 5 * tokens // (2 * experts)
    scale_factor = HEAD_DIM ** (-0.5)
    turn = orders(dp_size)

    routes_all = gather_expert(routes.T)
    gates_all = gather_expert(gate_weights.T)
    time_group = gather_expert(time_embed).reshape(experts * latents, model_width)
    cot_all = gather_expert(cotangent)
    time_all = gather_dp(gather_ordered(time_embed))

    named = routes_all == expert_index
    member = jnp.any(named, axis=1)
    gate_here = jnp.sum(jnp.where(named, gates_all, 0.0), axis=1)
    position = jnp.arange(tokens, dtype=jnp.int32)
    before = (position[:, None] < position[None, :]).astype(jnp.bfloat16)
    slot = jnp.dot(
        member.astype(jnp.bfloat16), before, preferred_element_type=jnp.float32
    ).astype(jnp.int32)
    slot = jnp.where(member, slot, capacity)
    pick = (
        slot[:, None, :] == jnp.arange(capacity, dtype=jnp.int32)[None, :, None]
    ).astype(jnp.bfloat16)
    local_counts = jnp.sum(
        (routes[:, :, None] == jnp.arange(experts, dtype=jnp.int32)).astype(jnp.int32),
        axis=(0, 1),
    )

    cond_group = jax.nn.silu(time_group.astype(jnp.float32)).astype(jnp.bfloat16)
    mod_group = jnp.dot(cond_group, ada_weight, preferred_element_type=jnp.float32) + ada_bias
    modulation = mod_group[:latents]
    shift_one, scale_one, gate_one, shift_two, scale_two, gate_two = jnp.split(
        modulation, 6, axis=1
    )
    gate_two_group = mod_group[:, 5 * model_width :].reshape(experts, latents, 1, model_width)
    residual_in = patches.astype(jnp.float32).reshape(latents, seq_len, model_width)
    first_full, first_pull = jax.vjp(modulate, residual_in, shift_one, scale_one)
    first_in = first_full.reshape(tokens, model_width).astype(jnp.bfloat16)
    qkv_all = jnp.dot(first_in, qkv_weight, preferred_element_type=jnp.float32).astype(jnp.bfloat16)
    head_shape = (latents, seq_len, head_count, HEAD_DIM)
    queries = qkv_all[:, :model_width].reshape(head_shape)
    keys_all = qkv_all[:, model_width : 2 * model_width].reshape(head_shape)
    values_all = qkv_all[:, 2 * model_width :].reshape(head_shape)
    scores = (
        jnp.einsum("bqhd,bkhd->bhqk", queries, keys_all, preferred_element_type=jnp.float32)
        * scale_factor
    )
    row_peak = jnp.max(scores, axis=-1, keepdims=True)
    shifted_exp = jnp.exp(scores - row_peak)
    row_total = jnp.sum(shifted_exp, axis=-1, keepdims=True)
    log_total = row_peak + jnp.log(row_total)
    probs_low = (shifted_exp / row_total).astype(jnp.bfloat16)
    attended = jnp.einsum(
        "bhqk,bkhd->bqhd", probs_low, values_all, preferred_element_type=jnp.float32
    )
    attended = attended.reshape(tokens, model_width).astype(jnp.bfloat16)
    attn_proj = jnp.dot(attended, out_weight, preferred_element_type=jnp.float32).reshape(
        latents, seq_len, model_width
    )
    middle = residual_in + gate_one[:, None, :] * attn_proj
    second_full, second_pull = jax.vjp(modulate, middle, shift_two, scale_two)
    second_in = second_full.reshape(tokens, model_width).astype(jnp.bfloat16)
    second_all = gather_expert(second_in)

    shared_pre = jnp.dot(second_in, up_weight, preferred_element_type=jnp.float32)
    shared_act = gelu_tanh(shared_pre).astype(jnp.bfloat16)
    shared_out = jnp.dot(shared_act, down_weight, preferred_element_type=jnp.float32)
    grad_result = cotangent.astype(jnp.float32).reshape(latents, seq_len, model_width)
    grad_branch = (gate_two[:, None, :] * grad_result).reshape(tokens, model_width)
    grad_shared = grad_branch.astype(jnp.bfloat16)
    grad_w_down = contract_rows(shared_act, grad_shared)
    sum_w_down = sum_over_all(grad_w_down, turn[0])
    grad_shared_act = project_back(grad_shared, down_weight)
    grad_shared_pre = (grad_shared_act * gelu_slope(shared_pre)).astype(jnp.bfloat16)
    grad_w_up = contract_rows(second_in, grad_shared_pre)
    sum_w_up = sum_over_all(grad_w_up, turn[1])
    grad_second = project_back(grad_shared_pre, up_weight)

    up_matrix = expert_up[0]
    down_matrix = expert_down[0]
    grad_branch_all = (
        gate_two_group
        * cot_all.astype(jnp.float32).reshape(experts, latents, seq_len, model_width)
    ).reshape(experts, tokens, model_width)
    grad_pair_all = (gate_here[:, :, None] * grad_branch_all).astype(jnp.bfloat16)

    def to_slots(values_in):
        return (
            jnp.einsum("bct,btd->bcd", pick, values_in, preferred_element_type=jnp.float32)
            .astype(jnp.bfloat16)
            .reshape(experts * capacity, model_width)
        )

    def to_tokens(values_in):
        return jnp.einsum(
            "bct,bcd->btd",
            pick,
            values_in.reshape(experts, capacity, model_width),
            preferred_element_type=jnp.float32,
        )

    grad_rows_out = to_slots(grad_pair_all)
    rows_in = to_slots(second_all)
    pre_act = jnp.dot(rows_in, up_matrix, preferred_element_type=jnp.float32)
    act_rows = gelu_tanh(pre_act).astype(jnp.bfloat16)
    grad_e_act = project_back(grad_rows_out, down_matrix)
    grad_e_pre = (grad_e_act * gelu_slope(pre_act)).astype(jnp.bfloat16)
    grad_e_up = contract_rows(rows_in, grad_e_pre)
    sum_e_up = sum_over_dp(grad_e_up, turn[2])
    grad_rows_in = project_back(grad_e_pre, up_matrix).astype(jnp.bfloat16)
    grad_tokens = to_tokens(grad_rows_in)
    grad_second = grad_second + scatter_expert({r: grad_tokens[r] for r in range(experts)})
    grad_e_down = contract_rows(act_rows, grad_rows_out)
    sum_e_down = sum_over_dp(grad_e_down, turn[0])
    out_rows = jnp.dot(act_rows, down_matrix, preferred_element_type=jnp.float32).astype(
        jnp.bfloat16
    )
    mixture_parts = gate_here[:, :, None] * to_tokens(out_rows)
    mixture = scatter_expert({r: mixture_parts[r] for r in range(experts)})

    branch = (shared_out + mixture).reshape(latents, seq_len, model_width)
    result = middle + gate_two[:, None, :] * branch
    block_out = result.reshape(tokens, model_width).astype(jnp.bfloat16)
    grad_gate_two = jnp.sum(grad_result * branch, axis=1)

    grad_mid_norm, grad_shift_two, grad_scale_two = second_pull(
        grad_second.reshape(latents, seq_len, model_width)
    )
    grad_middle = grad_result + grad_mid_norm
    grad_gate_one = jnp.sum(grad_middle * attn_proj, axis=1)
    grad_attn = (
        (gate_one[:, None, :] * grad_middle).reshape(tokens, model_width).astype(jnp.bfloat16)
    )
    grad_w_out = contract_rows(attended, grad_attn)
    sum_w_out = sum_over_all(grad_w_out, turn[1])
    grad_attended = project_back(grad_attn, out_weight).astype(jnp.bfloat16).reshape(head_shape)
    scores_again = (
        jnp.einsum("bqhd,bkhd->bhqk", queries, keys_all, preferred_element_type=jnp.float32)
        * scale_factor
    )
    attn_probs = jnp.exp(scores_again - log_total)
    probs_again = attn_probs.astype(jnp.bfloat16)
    grad_values = jnp.einsum(
        "bhqk,bqhd->bkhd", probs_again, grad_attended, preferred_element_type=jnp.float32
    )
    grad_probs = jnp.einsum(
        "bqhd,bkhd->bhqk", grad_attended, values_all, preferred_element_type=jnp.float32
    )
    grad_scores = (
        attn_probs * (grad_probs - jnp.sum(attn_probs * grad_probs, axis=-1, keepdims=True))
    ).astype(jnp.bfloat16)
    grad_queries = (
        jnp.einsum("bhqk,bkhd->bqhd", grad_scores, keys_all, preferred_element_type=jnp.float32)
        * scale_factor
    )
    grad_keys = (
        jnp.einsum("bhqk,bqhd->bkhd", grad_scores, queries, preferred_element_type=jnp.float32)
        * scale_factor
    )
    grad_qkv_rows = jnp.concatenate(
        [
            grad_queries.reshape(tokens, model_width),
            grad_keys.reshape(tokens, model_width),
            grad_values.reshape(tokens, model_width),
        ],
        axis=1,
    ).astype(jnp.bfloat16)
    grad_w_qkv = contract_rows(first_in, grad_qkv_rows)
    sum_w_qkv = sum_over_all(grad_w_qkv, turn[2])
    grad_first = project_back(grad_qkv_rows, qkv_weight)
    grad_in_norm, grad_shift_one, grad_scale_one = first_pull(
        grad_first.reshape(latents, seq_len, model_width)
    )
    grad_input = (grad_middle + grad_in_norm).reshape(tokens, model_width)

    count_parts = jnp.concatenate([local_counts // 128, local_counts % 128]).astype(jnp.bfloat16)
    count_rows = jnp.zeros((latents, 128), jnp.bfloat16).at[0, : 2 * experts].set(count_parts)
    early = jnp.concatenate(
        [
            grad_gate_one.astype(jnp.bfloat16),
            grad_shift_two.astype(jnp.bfloat16),
            grad_scale_two.astype(jnp.bfloat16),
            grad_gate_two.astype(jnp.bfloat16),
            count_rows,
        ],
        axis=1,
    )
    late = jnp.concatenate(
        [grad_shift_one.astype(jnp.bfloat16), grad_scale_one.astype(jnp.bfloat16)], axis=1
    )

    def gather_all(value):
        return gather_dp(gather_ordered(value))

    early_all = gather_all(early)
    late_all = gather_all(late)
    grad_mod_all = jnp.concatenate([late_all, early_all[:, : 4 * model_width]], axis=1)
    count_sums = jnp.sum(early_all[:, 4 * model_width :].astype(jnp.float32), axis=0).astype(
        jnp.int32
    )
    counts = count_sums[:experts] * 128 + count_sums[experts : 2 * experts]
    cond_all = jax.nn.silu(time_all.astype(jnp.float32)).astype(jnp.bfloat16)
    ada_rows = model_width // dp_size
    cond_mine = lax.dynamic_slice_in_dim(cond_all.T, dp_index * ada_rows, ada_rows, axis=0)
    sum_ada = jnp.dot(cond_mine, grad_mod_all, preferred_element_type=jnp.float32)
    bias_all = jnp.sum(grad_mod_all.astype(jnp.float32), axis=0)
    bias_size = bias_all.shape[0] // dp_size
    sum_bias = lax.dynamic_slice_in_dim(bias_all, dp_index * bias_size, bias_size)
    return (
        block_out,
        grad_input,
        sum_ada,
        sum_bias,
        sum_w_qkv,
        sum_w_out,
        sum_w_up,
        sum_w_down,
        sum_e_up.astype(jnp.float32)[None],
        sum_e_down.astype(jnp.float32)[None],
        counts,
    )


def solution(mesh):
    in_specs = (
        P(("dp", "expert"), None),
        P(("dp", "expert"), None),
        P(),
        P(),
        P(),
        P(),
        P(),
        P(),
        P("expert", None, None),
        P("expert", None, None),
        P(("dp", "expert"), None),
        P(("dp", "expert"), None),
        P(("dp", "expert"), None),
    )
    out_specs = (
        P(("dp", "expert"), None),
        P(("dp", "expert"), None),
        P("dp", None),
        P("dp"),
        P("dp", None),
        P("dp", None),
        P("dp", None),
        P("dp", None),
        P("expert", "dp", None),
        P("expert", "dp", None),
        P(),
    )
    return jax.shard_map(
        on_device, mesh=mesh, in_specs=in_specs, out_specs=out_specs, check_vma=False
    )
```

time: 980 us -> 561 us (0.57)
  the two profiles are of different devices: /device:TPU:0 before, /device:TPU:8 now
where the time goes in v1:
time: 561 us; the launch traced here: 552 us
  matrix products  153 us (27%)
  waiting for transfers between devices  147 us (26%)
  other arithmetic  94.2 us (17%)
  local copies, waits for them, and re-layouts  78.3 us (14%)
  starting transfers between devices  77.2 us (14%)
    ppermute x27, waiting for transfers between devices, swap_dp(): lax.ppermute(value, 'dp', [(i, index_of(label_of(i) ^ 1 << bit)) for i in...  101 us
    ppermute x27, starting transfers between devices, swap_dp(): lax.ppermute(value, 'dp', [(i, index_of(label_of(i) ^ 1 << bit)) for i in...  61.7 us
    dot_general x6, matrix products, project_back(): lax.dot_general(left_in, right_in, (((1,), (1,)), ((), ())), preferred_el...  45.9 us
    ppermute x38, waiting for transfers between devices, swap_expert(): lax.ppermute(value, 'expert', [(i, i ^ 1 << bit) for i in range(size)])  45.6 us
    dot_general x6, matrix products, contract_rows(): lax.dot_general(left_in, right_in, (((0,), (0,)), ((), ())), preferred_el...  36.6 us
    another operation x24, other arithmetic, scatter_dp(): away = jnp.stack([shards[r | 1 << bit] for r in low])  26.3 us
    unnamed x217, local copies, waits for them, and re-layouts  18.4 us
    concatenate x3, local copies, waits for them, and re-layouts, gather_dp(): value = jnp.concatenate([value, swap_dp(value, bit)], axis=0)  16.5 us
  transfers between devices with their start and end apart: 65, of which 26 were waited for; matrix products, arithmetic and copies ran while one was open for 57% of the time, Pallas kernels for 0%

profile of v1, /device:TPU:8, one launch (start us, length us, event | category | flops | bytes accessed | tf_op | source)
XLA Modules:
  0.0 551.9 jit_solution(16204647557352102176)
XLA Ops:
  15.6 4.1 convolution_add_fusion
  59.2 4.9 fusion.196
  64.1 5.5 fusion.27
  76.9 4.0 convolution_convert_fusion.3
  112.3 4.7 concatenate.101
  126.6 9.8 %fusion.38 = f32[1280,3072]{1,0:T(8,128)} fusion(bf16[1280,768]{1,0:T(8,128)(2,1)S(1)} %bitcast.548, bf16[1,768,3072]{2,1,0:T(8,128)(2,1)S(1)} %bitcast.545), kind=kOutput, calls=%fused_computation.59 | convolution fusion | flops 6039797760 | bytes 22413312 | tf_op jit(solution)/shard_map/dot_general | solution.py:295
  136.4 13.7 %fusion.44 = bf16[1280,768]{1,0:T(8,128)(2,1)} fusion(bf16[1,3072,768]{2,1,0:T(8,128)(2,1)S(1)} %bitcast.543, f32[1280,3072]{1,0:T(8,128)} %fusion.38), kind=kOutput, calls=%fused_computation.67 | convolution fusion | flops 6076170240 | bytes 22413312 | tf_op jit(solution)/shard_map/dot_general | solution.py:306
  150.1 11.7 %convolution_convert_fusion = bf16[3072,768]{1,0:T(8,128)(2,1)S(1)} fusion(bf16[1280,768]{1,0:T(8,128)(2,1)S(1)} %bitcast.546, f32[1280,3072]{1,0:T(8,128)} %fusion.38), kind=kOutput, calls=%fused_computation.49 | convolution fusion | flops 6077546496 | bytes 22413312 | tf_op jit(solution)/shard_map/dot_general | solution.py:38
  161.8 21.3 %fusion.12 = bf16[1280,3072]{1,0:T(8,128)(2,1)} fusion(f32[1280,3072]{1,0:T(8,128)} %fusion.38, bf16[1280,768]{1,0:T(8,128)(2,1)} %bitcast.547, bf16[1,3072,768]{2,1,0:T(8,128)(2,1)} %param.24), kind=kOutput, calls=%fused_computation.16 | convolution fusion | flops 6110576640 | bytes 30277632 | tf_op jit(solution)/shard_map/dot_general | solution.py:44
  183.1 10.2 %fusion.41 = bf16[1280,768]{1,0:T(8,128)(2,1)S(1)} fusion(bf16[1280,3072]{1,0:T(8,128)(2,1)} %fusion.12, bf16[1,768,3072]{2,1,0:T(8,128)(2,1)} %param.23), kind=kOutput, calls=%fused_computation.66 | convolution fusion | flops 6040780800 | bytes 14548992 | tf_op jit(solution)/shard_map/dot_general | solution.py:44
  193.3 10.4 %convolution_convert_fusion.1 = bf16[768,3072]{1,0:T(8,128)(2,1)S(1)} fusion(bf16[1280,768]{1,0:T(8,128)(2,1)S(1)} %bitcast.549, bf16[1280,3072]{1,0:T(8,128)(2,1)} %fusion.12), kind=kOutput, calls=%fused_computation.50 | convolution fusion | flops 6042157056 | bytes 14548992 | tf_op jit(solution)/shard_map/dot_general | solution.py:38
  226.6 26.7 %collective-permute-done.20 = bf16[512,768]{1,0:T(8,128)(2,1)S(1)} collective-permute-done((bf16[512,768]{1,0:T(8,128)(2,1)S(1)}, bf16[512,768]{1,0:T(8,128)(2,1)S(1)}, u32[]{:S(2)}, u32[]{:S(2)}) %collective-permute-start.20) | collective-permute-done | bytes 786464 | tf_op jit(solution)/shard_map/ppermute | solution.py:76
  253.3 4.4 collective-permute-start.48
  273.9 4.3 fusion.94
  278.3 7.2 %multiply_reduce_fusion = (f32[2,12,256]{2,1,0:T(8,128)S(1)}, f32[2,12,256,256]{2,3,1,0:T(8,128)}) fusion(f32[2,12,256,256]{2,3,1,0:T(8,128)} %copy-done.1, f32[2,12,256]{2,1,0:T(8,128)S(1)} %copy-done.42, bf16[2,256,12,64]{1,0,3,2:T(2,128)(2,1)S(1)} %copy-done.25, bf16[2,256,12,64]{1,0,3,2:T(2,128)(2,1)S(1)} %copy-done.15), kind=kOutput, calls=%fused_computation.42 | convolution fusion | flops 207611904 | bytes 14204928 | tf_op jit(solution)/shard_map/bqhd,bkhd->bhqk/dot_general | solution.py:337
  285.5 4.6 multiply_convert_fusion
  300.5 6.2 %convolution_convert_fusion.4 = bf16[768,2304]{1,0:T(8,128)(2,1)} fusion(bf16[512,768]{1,0:T(8,128)(2,1)} %copy-done.34, bf16[512,2304]{0,1:T(8,128)(2,1)} %copy-done.21), kind=kOutput, calls=%fused_computation.53 | convolution fusion | flops 1813708800 | bytes 6684672 | tf_op jit(solution)/shard_map/dot_general | solution.py:38
  312.3 4.7 bitcast_reduce_fusion
  334.0 4.8 collective-permute-done.29
  340.9 5.6 %concatenate.107 = bf16[64,1536]{1,0:T(8,128)(2,1)} concatenate(bf16[4,1536]{1,0:T(4,128)(2,1)} %copy-done.44, bf16[4,1536]{1,0:T(4,128)(2,1)S(1)} %get-tuple-element.133, bf16[8,1536]{1,0:T(8,128)(2,1)} %copy-done.46, bf16[16,1536]{1,0:T(8,128)(2,1)} %copy-done.48, bf16[32,1536]{1,0:T(8,128)(2,1)} %copy-done.55), dimensions={0} | concatenate | bytes 393216 | tf_op jit(solution)/shard_map/concatenate | solution.py:115
  352.7 8.3 %collective-permute-done.34 = bf16[32,3200]{1,0:T(8,128)(2,1)S(1)} collective-permute-done((bf16[32,3200]{1,0:T(8,128)(2,1)S(1)}, bf16[32,3200]{1,0:T(8,128)(2,1)S(1)}, u32[]{:S(2)}, u32[]{:S(2)}) %collective-permute-start.34) | collective-permute-done | bytes 204832 | tf_op jit(solution)/shard_map/ppermute | solution.py:69
  361.6 6.2 %concatenate.116 = bf16[64,3200]{1,0:T(8,128)(2,1)} concatenate(bf16[4,3200]{1,0:T(4,128)(2,1)} %copy-done.40, bf16[4,3200]{1,0:T(4,128)(2,1)} %copy-done.39, bf16[8,3200]{1,0:T(8,128)(2,1)} %copy-done.43, bf16[16,3200]{1,0:T(8,128)(2,1)} %collective-permute-done.33, bf16[32,3200]{1,0:T(8,128)(2,1)} %copy-done.47), dimensions={0} | concatenate | bytes 819200 | tf_op jit(solution)/shard_map/concatenate | solution.py:115
  382.5 14.5 %collective-permute-done.42 = bf16[4,96,384]{2,1,0:T(8,128)(2,1)S(1)} collective-permute-done((bf16[4,96,384]{2,1,0:T(8,128)(2,1)S(1)}, bf16[4,96,384]{2,1,0:T(8,128)(2,1)S(1)}, u32[]{:S(2)}, u32[]{:S(2)}) %collective-permute-start.42) | collective-permute-done | bytes 294944 | tf_op jit(solution)/shard_map/ppermute | solution.py:69
  400.9 7.3 %collective-permute-done.43 = bf16[2,96,384]{2,1,0:T(8,128)(2,1)S(1)} collective-permute-done((bf16[2,96,384]{2,1,0:T(8,128)(2,1)S(1)}, bf16[2,96,384]{2,1,0:T(8,128)(2,1)S(1)}, u32[]{:S(2)}, u32[]{:S(2)}) %collective-permute-start.43) | collective-permute-done | bytes 147488 | tf_op jit(solution)/shard_map/ppermute | solution.py:69
  410.0 16.4 %collective-permute-done.44 = bf16[1,96,384]{2,1,0:T(8,128)(2,1)S(1)} collective-permute-done((bf16[1,96,384]{2,1,0:T(8,128)(2,1)S(1)}, bf16[1,96,384]{2,1,0:T(8,128)(2,1)S(1)}, u32[]{:S(2)}, u32[]{:S(2)}) %collective-permute-start.44) | collective-permute-done | bytes 73760 | tf_op jit(solution)/shard_map/ppermute | solution.py:69
  436.0 4.6 collective-permute-done.56
  448.9 6.1 %collective-permute-done.51 = bf16[96,1536]{1,0:T(8,128)(2,1)S(1)} collective-permute-done((bf16[96,1536]{1,0:T(8,128)(2,1)S(1)}, bf16[96,1536]{1,0:T(8,128)(2,1)S(1)}, u32[]{:S(2)}, u32[]{:S(2)}) %collective-permute-start.51) | collective-permute-done | bytes 294944 | tf_op jit(solution)/shard_map/ppermute | solution.py:76
  466.6 14.2 %collective-permute-done.36 = bf16[4,96,1152]{2,1,0:T(8,128)(2,1)} collective-permute-done((bf16[4,96,1152]{2,1,0:T(8,128)(2,1)}, bf16[4,96,1152]{2,1,0:T(8,128)(2,1)}, u32[]{:S(2)}, u32[]{:S(2)}) %collective-permute-start.36) | collective-permute-done | bytes 884768 | tf_op jit(solution)/shard_map/ppermute | solution.py:69
  484.5 24.5 %collective-permute-start.61 = (bf16[1,96,3072]{2,1,0:T(8,128)(2,1)S(1)}, bf16[1,96,3072]{2,1,0:T(8,128)(2,1)S(1)}, u32[]{:S(2)}, u32[]{:S(2)}) collective-permute-start(bf16[1,96,3072]{2,1,0:T(8,128)(2,1)S(1)} %fusion.126), channel_id=1, source_target_pairs={{0,8},{4,12},{8,0},{12,4},{16,24},{20,28},{24,16},{28,20},{1,9},{5... | collective-permute-start | bytes 1769480 | tf_op jit(solution)/shard_map/ppermute | solution.py:69
  510.2 9.6 %collective-permute-start.38 = (bf16[1,96,1152]{2,1,0:T(8,128)(2,1)S(1)}, bf16[1,96,1152]{2,1,0:T(8,128)(2,1)S(1)}, u32[]{:S(2)}, u32[]{:S(2)}) collective-permute-start(bf16[1,96,1152]{2,1,0:T(8,128)(2,1)S(1)} %fusion.165), channel_id=1, source_target_pairs={{0,8},{4,12},{8,0},{12,4},{16,24},{20,28},{24,16},{28,20},{1,9},{5... | collective-permute-start | bytes 663560 | tf_op jit(solution)/shard_map/ppermute | solution.py:69
  522.8 5.1 collective-permute-done.38
  535.3 12.6 %collective-permute-done.64 = bf16[1,384,768]{2,1,0:T(8,128)(2,1)S(1)} collective-permute-done((bf16[1,384,768]{2,1,0:T(8,128)(2,1)S(1)}, bf16[1,384,768]{2,1,0:T(8,128)(2,1)S(1)}, u32[]{:S(2)}, u32[]{:S(2)}) %collective-permute-start.64) | collective-permute-done | bytes 589856 | tf_op jit(solution)/shard_map/ppermute | solution.py:69
  (497 shorter events, 251.1 us)
Async XLA Ops:
  2.3 90.8 %collective-permute-start.3 = (s32[2,512]{1,0:T(2,128)}, s32[2,512]{1,0:T(2,128)}, u32[]{:S(2)}, u32[]{:S(2)}) collective-permute-start(s32[2,512]{1,0:T(2,128)} %bitcast.527), channel_id=1, source_target_pairs={{0,1},{1,0},{2,3},{3,2},{4,5},{5,4},{6,7},{7,6},{8,9},{9,8},{10,11... | collective-permute-start | bytes 12296 | tf_op jit(solution)/shard_map/ppermute | solution.py:76
  2.5 89.2 %collective-permute-start.4 = (s32[2,512]{1,0:T(2,128)}, s32[2,512]{1,0:T(2,128)}, u32[]{:S(2)}, u32[]{:S(2)}) collective-permute-start(s32[2,512]{1,0:T(2,128)} %bitcast.528), channel_id=1, source_target_pairs={{0,2},{1,3},{2,0},{3,1},{4,6},{5,7},{6,4},{7,5},{8,10},{9,11},{10,... | collective-permute-start | bytes 12296 | tf_op jit(solution)/shard_map/ppermute | solution.py:76
  3.0 90.0 %collective-permute-start.16 = (bf16[512,768]{1,0:T(8,128)(2,1)}, bf16[512,768]{1,0:T(8,128)(2,1)}, u32[]{:S(2)}, u32[]{:S(2)}) collective-permute-start(bf16[512,768]{1,0:T(8,128)(2,1)} %param.27), channel_id=1, source_target_pairs={{0,2},{1,3},{2,0},{3,1},{4,6},{5,7},{6,4},{7,5},{8,10},{9,11},{10,... | collective-permute-start | bytes 2359304 | tf_op jit(solution)/shard_map/ppermute | solution.py:76
  12.4 79.4 %collective-permute-start.21 = (bf16[4,768]{1,0:T(4,128)(2,1)}, bf16[4,768]{1,0:T(4,128)(2,1)}, u32[]{:S(2)}, u32[]{:S(2)}) collective-permute-start(bf16[4,768]{1,0:T(4,128)(2,1)} %pad_maximum_fusion.25), channel_id=1, source_target_pairs={{0,2},{1,3},{2,0},{3,1},{4,6},{5,7},{6,4},{7,5},{8,10},{9,11},{10,... | collective-permute-start | bytes 18440 | tf_op jit(solution)/shard_map/ppermute | solution.py:76
  53.9 48.0 %collective-permute-start.10 = (bf16[512,768]{1,0:T(8,128)(2,1)}, bf16[512,768]{1,0:T(8,128)(2,1)}, u32[]{:S(2)}, u32[]{:S(2)}) collective-permute-start(bf16[512,768]{1,0:T(8,128)(2,1)} %bitcast.10), channel_id=1, source_target_pairs={{0,2},{1,3},{2,0},{3,1},{4,6},{5,7},{6,4},{7,5},{8,10},{9,11},{10,... | collective-permute-start | bytes 2359304 | tf_op jit(solution)/shard_map/ppermute | solution.py:76
  91.7 26.9 %collective-permute-start.15 = (bf16[512,768]{1,0:T(8,128)(2,1)}, bf16[512,768]{1,0:T(8,128)(2,1)}, u32[]{:S(2)}, u32[]{:S(2)}) collective-permute-start(bf16[512,768]{1,0:T(8,128)(2,1)} %param.27), channel_id=1, source_target_pairs={{0,1},{1,0},{2,3},{3,2},{4,5},{5,4},{6,7},{7,6},{8,9},{9,8},{10,11... | collective-permute-start | bytes 2359304 | tf_op jit(solution)/shard_map/ppermute | solution.py:76
  93.0 26.1 %collective-permute-start.17 = (bf16[512,768]{1,0:T(8,128)(2,1)}, bf16[512,768]{1,0:T(8,128)(2,1)}, u32[]{:S(2)}, u32[]{:S(2)}) collective-permute-start(bf16[512,768]{1,0:T(8,128)(2,1)} %collective-permute-done.16), channel_id=1, source_target_pairs={{0,1},{1,0},{2,3},{3,2},{4,5},{5,4},{6,7},{7,6},{8,9},{9,8},{10,11... | collective-permute-start | bytes 2359304 | tf_op jit(solution)/shard_map/ppermute | solution.py:76
  98.3 24.3 %collective-permute-start.9 = (bf16[512,768]{1,0:T(8,128)(2,1)}, bf16[512,768]{1,0:T(8,128)(2,1)}, u32[]{:S(2)}, u32[]{:S(2)}) collective-permute-start(bf16[512,768]{1,0:T(8,128)(2,1)} %bitcast.10), channel_id=1, source_target_pairs={{0,1},{1,0},{2,3},{3,2},{4,5},{5,4},{6,7},{7,6},{8,9},{9,8},{10,11... | collective-permute-start | bytes 2359304 | tf_op jit(solution)/shard_map/ppermute | solution.py:76
  101.8 20.8 %collective-permute-start.11 = (bf16[512,768]{1,0:T(8,128)(2,1)}, bf16[512,768]{1,0:T(8,128)(2,1)}, u32[]{:S(2)}, u32[]{:S(2)}) collective-permute-start(bf16[512,768]{1,0:T(8,128)(2,1)} %collective-permute-done.10), channel_id=1, source_target_pairs={{0,1},{1,0},{2,3},{3,2},{4,5},{5,4},{6,7},{7,6},{8,9},{9,8},{10,11... | collective-permute-start | bytes 2359304 | tf_op jit(solution)/shard_map/ppermute | solution.py:76
  112.3 104.3 %collective-permute-start.53 = (bf16[3072,384]{0,1:T(8,128)(2,1)}, bf16[3072,384]{0,1:T(8,128)(2,1)}, u32[]{:S(2)}, u32[]{:S(2)}) collective-permute-start(bf16[3072,384]{0,1:T(8,128)(2,1)} %constant_dynamic-slice_fusion), channel_id=1, source_target_pairs={{0,1},{1,0},{2,3},{3,2},{4,5},{5,4},{6,7},{7,6},{8,9},{9,8},{10,11... | collective-permute-start | bytes 7077896 | tf_op jit(solution)/shard_map/ppermute | solution.py:76
  118.6 101.3 %collective-permute-start.47 = (bf16[768,1536]{1,0:T(8,128)(2,1)}, bf16[768,1536]{1,0:T(8,128)(2,1)S(1)}, u32[]{:S(2)}, u32[]{:S(2)}) collective-permute-start(bf16[768,1536]{1,0:T(8,128)(2,1)} %constant_dynamic-slice_fusion.1), channel_id=1, source_target_pairs={{0,1},{1,0},{2,3},{3,2},{4,5},{5,4},{6,7},{7,6},{8,9},{9,8},{10,11... | collective-permute-start | bytes 7077896 | tf_op jit(solution)/shard_map/ppermute | solution.py:76
  212.1 164.3 %collective-permute-start.59 = (bf16[4,96,3072]{2,1,0:T(8,128)(2,1)}, bf16[4,96,3072]{2,1,0:T(8,128)(2,1)}, u32[]{:S(2)}, u32[]{:S(2)}) collective-permute-start(bf16[4,96,3072]{2,1,0:T(8,128)(2,1)} %pad_maximum_fusion), channel_id=1, source_target_pairs={{0,24},{4,28},{8,16},{12,20},{16,8},{20,12},{24,0},{28,4},{1,25},{... | collective-permute-start | bytes 7077896 | tf_op jit(solution)/shard_map/ppermute | solution.py:69
  214.5 45.6 %collective-permute-start.12 = (bf16[512,768]{1,0:T(8,128)(2,1)S(1)}, bf16[512,768]{1,0:T(8,128)(2,1)S(1)}, u32[]{:S(2)}, u32[]{:S(2)}) collective-permute-start(bf16[512,768]{1,0:T(8,128)(2,1)S(1)} %get-tuple-element.89), channel_id=1, source_target_pairs={{0,1},{1,0},{2,3},{3,2},{4,5},{5,4},{6,7},{7,6},{8,9},{9,8},{10,11... | collective-permute-start | bytes 2359304 | tf_op jit(solution)/shard_map/ppermute | solution.py:76
  216.6 43.5 %collective-permute-start.14 = (bf16[512,768]{1,0:T(8,128)(2,1)S(1)}, bf16[512,768]{1,0:T(8,128)(2,1)S(1)}, u32[]{:S(2)}, u32[]{:S(2)}) collective-permute-start(bf16[512,768]{1,0:T(8,128)(2,1)S(1)} %fusion.77), channel_id=1, source_target_pairs={{0,2},{1,3},{2,0},{3,1},{4,6},{5,7},{6,4},{7,5},{8,10},{9,11},{10,... | collective-permute-start | bytes 2359304 | tf_op jit(solution)/shard_map/ppermute | solution.py:76
  219.9 33.4 %collective-permute-start.20 = (bf16[512,768]{1,0:T(8,128)(2,1)S(1)}, bf16[512,768]{1,0:T(8,128)(2,1)S(1)}, u32[]{:S(2)}, u32[]{:S(2)}) collective-permute-start(bf16[512,768]{1,0:T(8,128)(2,1)S(1)} %fusion.72), channel_id=1, source_target_pairs={{0,2},{1,3},{2,0},{3,1},{4,6},{5,7},{6,4},{7,5},{8,10},{9,11},{10,... | collective-permute-start | bytes 2359304 | tf_op jit(solution)/shard_map/ppermute | solution.py:76
  225.2 122.4 %collective-permute-start.54 = (bf16[4,384,384]{1,2,0:T(8,128)(2,1)}, bf16[4,384,384]{1,2,0:T(8,128)(2,1)}, u32[]{:S(2)}, u32[]{:S(2)}) collective-permute-start(bf16[4,384,384]{1,2,0:T(8,128)(2,1)} %pad_maximum_fusion.3), channel_id=1, source_target_pairs={{0,4},{4,0},{8,12},{12,8},{16,20},{20,16},{24,28},{28,24},{1,5},{5... | collective-permute-start | bytes 3538952 | tf_op jit(solution)/shard_map/ppermute | solution.py:69
  253.3 96.2 %collective-permute-start.48 = (bf16[4,96,1536]{2,1,0:T(8,128)(2,1)}, bf16[4,96,1536]{2,1,0:T(8,128)(2,1)}, u32[]{:S(2)}, u32[]{:S(2)}) collective-permute-start(bf16[4,96,1536]{2,1,0:T(8,128)(2,1)} %pad_maximum_fusion.2), channel_id=1, source_target_pairs={{0,8},{4,12},{8,0},{12,4},{16,24},{20,28},{24,16},{28,20},{1,9},{5... | collective-permute-start | bytes 3538952 | tf_op jit(solution)/shard_map/ppermute | solution.py:69
  330.2 16.3 %collective-permute-start.33 = (bf16[16,3200]{1,0:T(8,128)(2,1)}, bf16[16,3200]{1,0:T(8,128)(2,1)}, u32[]{:S(2)}, u32[]{:S(2)}) collective-permute-start(bf16[16,3200]{1,0:T(8,128)(2,1)} %pad_maximum_fusion.15), channel_id=1, source_target_pairs={{0,8},{4,12},{8,0},{12,4},{16,24},{20,28},{24,16},{28,20},{1,9},{5... | collective-permute-start | bytes 307208 | tf_op jit(solution)/shard_map/ppermute | solution.py:69
  339.4 58.2 %collective-permute-start.62 = (bf16[4,384,768]{2,1,0:T(8,128)(2,1)}, bf16[4,384,768]{2,1,0:T(8,128)(2,1)}, u32[]{:S(2)}, u32[]{:S(2)}) collective-permute-start(bf16[4,384,768]{2,1,0:T(8,128)(2,1)} %pad_maximum_fusion.1), channel_id=1, source_target_pairs={{0,4},{4,0},{8,12},{12,8},{16,20},{20,16},{24,28},{28,24},{1,5},{5... | collective-permute-start | bytes 7077896 | tf_op jit(solution)/shard_map/ppermute | solution.py:69
  346.5 28.2 %collective-permute-start.41 = (bf16[768,384]{1,0:T(8,128)(2,1)}, bf16[768,384]{1,0:T(8,128)(2,1)}, u32[]{:S(2)}, u32[]{:S(2)}) collective-permute-start(bf16[768,384]{1,0:T(8,128)(2,1)} %constant_dynamic-slice_fusion.2), channel_id=1, source_target_pairs={{0,1},{1,0},{2,3},{3,2},{4,5},{5,4},{6,7},{7,6},{8,9},{9,8},{10,11... | collective-permute-start | bytes 1769480 | tf_op jit(solution)/shard_map/ppermute | solution.py:76
  347.5 107.6 %collective-permute-start.35 = (bf16[768,1152]{1,0:T(8,128)(2,1)}, bf16[768,1152]{1,0:T(8,128)(2,1)}, u32[]{:S(2)}, u32[]{:S(2)}) collective-permute-start(bf16[768,1152]{1,0:T(8,128)(2,1)} %constant_dynamic-slice_fusion.3), channel_id=1, source_target_pairs={{0,1},{1,0},{2,3},{3,2},{4,5},{5,4},{6,7},{7,6},{8,9},{9,8},{10,11... | collective-permute-start | bytes 5308424 | tf_op jit(solution)/shard_map/ppermute | solution.py:76
  361.6 67.3 %collective-permute-start.55 = (bf16[2,384,384]{1,2,0:T(8,128)(2,1)}, bf16[2,384,384]{1,2,0:T(8,128)(2,1)}, u32[]{:S(2)}, u32[]{:S(2)}) collective-permute-start(bf16[2,384,384]{1,2,0:T(8,128)(2,1)} %pad_maximum_fusion.9), channel_id=1, source_target_pairs={{0,8},{4,12},{8,0},{12,4},{16,24},{20,28},{24,16},{28,20},{1,9},{5... | collective-permute-start | bytes 1769480 | tf_op jit(solution)/shard_map/ppermute | solution.py:69
  374.7 59.3 %collective-permute-start.49 = (bf16[2,96,1536]{2,1,0:T(8,128)(2,1)S(1)}, bf16[2,96,1536]{2,1,0:T(8,128)(2,1)S(1)}, u32[]{:S(2)}, u32[]{:S(2)}) collective-permute-start(bf16[2,96,1536]{2,1,0:T(8,128)(2,1)S(1)} %copy-done.41), channel_id=1, source_target_pairs={{0,24},{4,28},{8,16},{12,20},{16,8},{20,12},{24,0},{28,4},{1,25},{... | collective-permute-start | bytes 1769480 | tf_op jit(solution)/shard_map/ppermute | solution.py:69
  376.4 20.6 %collective-permute-start.42 = (bf16[4,96,384]{2,1,0:T(8,128)(2,1)S(1)}, bf16[4,96,384]{2,1,0:T(8,128)(2,1)S(1)}, u32[]{:S(2)}, u32[]{:S(2)}) collective-permute-start(bf16[4,96,384]{2,1,0:T(8,128)(2,1)S(1)} %pad_maximum_fusion.12), channel_id=1, source_target_pairs={{0,8},{4,12},{8,0},{12,4},{16,24},{20,28},{24,16},{28,20},{1,9},{5... | collective-permute-start | bytes 884744 | tf_op jit(solution)/shard_map/ppermute | solution.py:69
  397.0 85.9 %collective-permute-start.60 = (bf16[2,96,3072]{2,1,0:T(8,128)(2,1)}, bf16[2,96,3072]{2,1,0:T(8,128)(2,1)}, u32[]{:S(2)}, u32[]{:S(2)}) collective-permute-start(bf16[2,96,3072]{2,1,0:T(8,128)(2,1)} %pad_maximum_fusion.4), channel_id=1, source_target_pairs={{0,4},{4,0},{8,12},{12,8},{16,20},{20,16},{24,28},{28,24},{1,5},{5... | collective-permute-start | bytes 3538952 | tf_op jit(solution)/shard_map/ppermute | solution.py:69
  408.3 18.2 %collective-permute-start.44 = (bf16[1,96,384]{2,1,0:T(8,128)(2,1)S(1)}, bf16[1,96,384]{2,1,0:T(8,128)(2,1)S(1)}, u32[]{:S(2)}, u32[]{:S(2)}) collective-permute-start(bf16[1,96,384]{2,1,0:T(8,128)(2,1)S(1)} %fusion.175), channel_id=1, source_target_pairs={{0,4},{4,0},{8,12},{12,8},{16,20},{20,16},{24,28},{28,24},{1,5},{5... | collective-permute-start | bytes 221192 | tf_op jit(solution)/shard_map/ppermute | solution.py:69
  426.4 93.4 %collective-permute-start.63 = (bf16[2,384,768]{2,1,0:T(8,128)(2,1)}, bf16[2,384,768]{2,1,0:T(8,128)(2,1)}, u32[]{:S(2)}, u32[]{:S(2)}) collective-permute-start(bf16[2,384,768]{2,1,0:T(8,128)(2,1)} %pad_maximum_fusion.5), channel_id=1, source_target_pairs={{0,8},{4,12},{8,0},{12,4},{16,24},{20,28},{24,16},{28,20},{1,9},{5... | collective-permute-start | bytes 3538952 | tf_op jit(solution)/shard_map/ppermute | solution.py:69
  458.5 22.4 %collective-permute-start.36 = (bf16[4,96,1152]{2,1,0:T(8,128)(2,1)}, bf16[4,96,1152]{2,1,0:T(8,128)(2,1)}, u32[]{:S(2)}, u32[]{:S(2)}) collective-permute-start(bf16[4,96,1152]{2,1,0:T(8,128)(2,1)} %pad_maximum_fusion.6), channel_id=1, source_target_pairs={{0,24},{4,28},{8,16},{12,20},{16,8},{20,12},{24,0},{28,4},{1,25},{... | collective-permute-start | bytes 2654216 | tf_op jit(solution)/shard_map/ppermute | solution.py:69
  482.2 26.8 %collective-permute-start.37 = (bf16[2,96,1152]{2,1,0:T(8,128)(2,1)S(1)}, bf16[2,96,1152]{2,1,0:T(8,128)(2,1)S(1)}, u32[]{:S(2)}, u32[]{:S(2)}) collective-permute-start(bf16[2,96,1152]{2,1,0:T(8,128)(2,1)S(1)} %pad_maximum_fusion.10), channel_id=1, source_target_pairs={{0,4},{4,0},{8,12},{12,8},{16,20},{20,16},{24,28},{28,24},{1,5},{5... | collective-permute-start | bytes 1327112 | tf_op jit(solution)/shard_map/ppermute | solution.py:69
  484.5 45.0 %collective-permute-start.61 = (bf16[1,96,3072]{2,1,0:T(8,128)(2,1)S(1)}, bf16[1,96,3072]{2,1,0:T(8,128)(2,1)S(1)}, u32[]{:S(2)}, u32[]{:S(2)}) collective-permute-start(bf16[1,96,3072]{2,1,0:T(8,128)(2,1)S(1)} %fusion.126), channel_id=1, source_target_pairs={{0,8},{4,12},{8,0},{12,4},{16,24},{20,28},{24,16},{28,20},{1,9},{5... | collective-permute-start | bytes 1769480 | tf_op jit(solution)/shard_map/ppermute | solution.py:69
  510.2 17.8 %collective-permute-start.38 = (bf16[1,96,1152]{2,1,0:T(8,128)(2,1)S(1)}, bf16[1,96,1152]{2,1,0:T(8,128)(2,1)S(1)}, u32[]{:S(2)}, u32[]{:S(2)}) collective-permute-start(bf16[1,96,1152]{2,1,0:T(8,128)(2,1)S(1)} %fusion.165), channel_id=1, source_target_pairs={{0,8},{4,12},{8,0},{12,4},{16,24},{20,28},{24,16},{28,20},{1,9},{5... | collective-permute-start | bytes 663560 | tf_op jit(solution)/shard_map/ppermute | solution.py:69
  521.4 26.5 %collective-permute-start.64 = (bf16[1,384,768]{2,1,0:T(8,128)(2,1)S(1)}, bf16[1,384,768]{2,1,0:T(8,128)(2,1)S(1)}, u32[]{:S(2)}, u32[]{:S(2)}) collective-permute-start(bf16[1,384,768]{2,1,0:T(8,128)(2,1)S(1)} %fusion.131), channel_id=1, source_target_pairs={{0,24},{4,28},{8,16},{12,20},{16,8},{20,12},{24,0},{28,4},{1,25},{... | collective-permute-start | bytes 1769480 | tf_op jit(solution)/shard_map/ppermute | solution.py:69
  (136 other events, 942.8 us)

commit v2 on v1

v2 whole, which is shorter than its diff:
```python
import functools
import math

import jax
import jax.numpy as jnp
import numpy as np
from jax import lax
from jax.experimental import pallas as pl
from jax.experimental.pallas import tpu as pltpu
from jax.sharding import PartitionSpec as P

HEAD_DIM = 64
VMEM_BYTES = 56 << 20
PARTS = 3
SQRT_TWO_OVER_PI = math.sqrt(2.0 / math.pi)


def nt(a,b): return lax.dot_general(a,b,(((1,),(1,)),((),())),preferred_element_type=jnp.float32)
def nn(a,b): return lax.dot_general(a,b,(((1,),(0,)),((),())),preferred_element_type=jnp.float32)
def tn(a,b): return lax.dot_general(a,b,(((0,),(0,)),((),())),preferred_element_type=jnp.float32)

def normalized(values_in):
    row_mean = jnp.mean(values_in, axis=-1, keepdims=True)
    centered = values_in - row_mean
    row_var = jnp.mean(centered * centered, axis=-1, keepdims=True)
    inverse = lax.rsqrt(row_var + 1e-06)
    return centered * inverse, inverse

def norm_back(grad_out, scale, normal, inverse):
    inner = grad_out * (1.0 + scale)
    mean_inner = jnp.mean(inner, axis=-1, keepdims=True)
    mean_cross = jnp.mean(inner * normal, axis=-1, keepdims=True)
    return inverse * (inner - mean_inner - normal * mean_cross)

def head_lanes(pair, head):
    lane = lax.broadcasted_iota(jnp.int32, pair.shape, 1)
    return jnp.where(lane // HEAD_DIM == head, pair, jnp.zeros_like(pair))

def attn_forward_kernel(x_ref, mod_ref, wqkv_ref, wout_ref, first_ref, qkv_ref, lse_ref, att_ref, proj_ref, second_ref):
    width = x_ref.shape[1]
    x = x_ref[...].astype(jnp.float32)
    mod = mod_ref[0]
    normal, _ = normalized(x)
    first_ref[...] = (normal * (1.0 + mod[1:2]) + mod[0:1]).astype(jnp.bfloat16)
    qkv_ref[...] = nn(first_ref[...], wqkv_ref[...]).astype(jnp.bfloat16)
    lane = 2 * HEAD_DIM
    for pair in range(width // lane):
        q2 = qkv_ref[:, pair * lane : (pair + 1) * lane]
        k2 = qkv_ref[:, width + pair * lane : width + (pair + 1) * lane]
        v2 = qkv_ref[:, 2 * width + pair * lane : 2 * width + (pair + 1) * lane]
        v2t = v2.T
        outs = []
        for head in range(2):
            scores = nt(head_lanes(k2, head), q2) * HEAD_DIM ** (-0.5)
            peak = jnp.max(scores, axis=0, keepdims=True)
            powers = jnp.exp(scores - peak)
            total = jnp.sum(powers, axis=0, keepdims=True)
            lse_ref[0, 2 * pair + head : 2 * pair + head + 1, :] = peak + jnp.log(total)
            probs = (powers * (1.0 / total)).astype(jnp.bfloat16)
            outs.append(nn(v2t[head * HEAD_DIM : (head + 1) * HEAD_DIM], probs))
        both = jnp.concatenate(outs, axis=0).astype(jnp.bfloat16)
        att_ref[:, pair * lane : (pair + 1) * lane] = both.T
    proj = nn(att_ref[...], wout_ref[...])
    proj_ref[...] = proj
    middle = x + mod[2:3] * proj
    normal2, _ = normalized(middle)
    second_ref[...] = (normal2 * (1.0 + mod[4:5]) + mod[3:4]).astype(jnp.bfloat16)

def attn_forward(patches, mod, wqkv, wout):
    tokens, width = patches.shape
    latents = mod.shape[0]
    seq = tokens // latents
    heads = width // HEAD_DIM
    rows = lambda cols: pl.BlockSpec((seq, cols), lambda i: (i, 0))
    whole = lambda a: pl.BlockSpec(a.shape, lambda i: (0, 0), pipeline_mode=pl.Buffered(1))
    return pl.pallas_call(
        attn_forward_kernel, grid=(latents,),
        in_specs=[rows(width), pl.BlockSpec((1,) + mod.shape[1:], lambda i: (i, 0, 0)), whole(wqkv), whole(wout)],
        out_specs=[rows(width), rows(3 * width), pl.BlockSpec((1, heads, seq), lambda i: (i, 0, 0)), rows(width), rows(width), rows(width)],
        out_shape=[jax.ShapeDtypeStruct((tokens, width), jnp.bfloat16), jax.ShapeDtypeStruct((tokens, 3 * width), jnp.bfloat16),
            jax.ShapeDtypeStruct((latents, heads, seq), jnp.float32), jax.ShapeDtypeStruct((tokens, width), jnp.bfloat16),
            jax.ShapeDtypeStruct((tokens, width), jnp.float32), jax.ShapeDtypeStruct((tokens, width), jnp.bfloat16)],
        compiler_params=pltpu.CompilerParams(vmem_limit_bytes=VMEM_BYTES))(patches, mod, wqkv, wout)

def attn_backward_kernel(extra, x_ref, mod_ref, proj_ref, qkv_ref, lse_ref, cot_ref, wout_ref, *rest):
    adds = rest[:extra]
    gqkv_ref, gattn_ref, gmid_ref, gmod_ref = rest[extra:]
    width = x_ref.shape[1]
    x = x_ref[...].astype(jnp.float32)
    mod = mod_ref[0]
    proj = proj_ref[...]
    normal, inverse = normalized(x + mod[2:3] * proj)
    grad_second = adds[0][...].astype(jnp.float32)
    for a in adds[1:]:
        grad_second = grad_second + a[...].astype(jnp.float32)
    gmod_ref[0, 1:2, :] = jnp.sum(grad_second, axis=0, keepdims=True)
    gmod_ref[0, 2:3, :] = jnp.sum(grad_second * normal, axis=0, keepdims=True)
    grad_middle = cot_ref[...].astype(jnp.float32) + norm_back(grad_second, mod[4:5], normal, inverse)
    gmid_ref[...] = grad_middle
    gmod_ref[0, 0:1, :] = jnp.sum(grad_middle * proj, axis=0, keepdims=True)
    gattn_ref[...] = (mod[2:3] * grad_middle).astype(jnp.bfloat16)
    grad_att = nt(gattn_ref[...], wout_ref[...]).astype(jnp.bfloat16)
    lane = 2 * HEAD_DIM
    scale = HEAD_DIM ** (-0.5)
    for pair in range(width // lane):
        sl = slice(pair * lane, (pair + 1) * lane)
        q2 = qkv_ref[:, pair * lane : (pair + 1) * lane]
        k2 = qkv_ref[:, width + pair * lane : width + (pair + 1) * lane]
        v2 = qkv_ref[:, 2 * width + pair * lane : 2 * width + (pair + 1) * lane]
        do2 = grad_att[:, sl]
        k2t = k2.T
        gq, gk, gv = [], [], []
        for head in range(2):
            scores = nt(head_lanes(k2, head), q2) * scale
            probs = jnp.exp(scores - lse_ref[0, 2 * pair + head : 2 * pair + head + 1, :])
            grad_probs = nt(head_lanes(v2, head), do2)
            inner = jnp.sum(probs * grad_probs, axis=0, keepdims=True)
            grad_scores = (probs * (grad_probs - inner)).astype(jnp.bfloat16)
            gv.append(nn(probs.astype(jnp.bfloat16), do2))
            gk.append(nn(grad_scores, q2))
            gq.append(nn(k2t[head * HEAD_DIM : (head + 1) * HEAD_DIM], grad_scores))
        low = lax.broadcasted_iota(jnp.int32, gv[0].shape, 1) < HEAD_DIM
        gqt = (jnp.concatenate(gq, axis=0) * scale).astype(jnp.bfloat16)
        gqkv_ref[:, pair * lane : (pair + 1) * lane] = gqt.T
        gqkv_ref[:, width + pair * lane : width + (pair + 1) * lane] = (jnp.where(low, gk[0], gk[1]) * scale).astype(jnp.bfloat16)
        gqkv_ref[:, 2 * width + pair * lane : 2 * width + (pair + 1) * lane] = jnp.where(low, gv[0], gv[1]).astype(jnp.bfloat16)

def attn_backward(patches, mod, proj, qkv, lse, cot, wout, adds):
    tokens, width = patches.shape
    latents = mod.shape[0]
    seq = tokens // latents
    rows = lambda cols: pl.BlockSpec((seq, cols), lambda i: (i, 0))
    per = lambda a: pl.BlockSpec((1,) + a.shape[1:], lambda i: (i, 0, 0))
    whole = lambda a: pl.BlockSpec(a.shape, lambda i: (0, 0), pipeline_mode=pl.Buffered(1))
    return pl.pallas_call(
        functools.partial(attn_backward_kernel, len(adds)), grid=(latents,),
        in_specs=[rows(width), per(mod), rows(width), rows(3 * width), per(lse), rows(width), whole(wout)] + [rows(width)] * len(adds),
        out_specs=[rows(3 * width), rows(width), rows(width), pl.BlockSpec((1, 3, width), lambda i: (i, 0, 0))],
        out_shape=[jax.ShapeDtypeStruct((tokens, 3 * width), jnp.bfloat16), jax.ShapeDtypeStruct((tokens, width), jnp.bfloat16),
            jax.ShapeDtypeStruct((tokens, width), jnp.float32), jax.ShapeDtypeStruct((latents, 3, width), jnp.float32)],
        compiler_params=pltpu.CompilerParams(vmem_limit_bytes=VMEM_BYTES))(patches, mod, proj, qkv, lse, cot, wout, *adds)

def input_backward_kernel(x_ref, mod_ref, gqkv_ref, gmid_ref, wqkv_ref, gin_ref, gmod_ref):
    mod = mod_ref[0]
    normal, inverse = normalized(x_ref[...].astype(jnp.float32))
    grad_first = nt(gqkv_ref[...], wqkv_ref[...])
    gmod_ref[0, 0:1, :] = jnp.sum(grad_first, axis=0, keepdims=True)
    gmod_ref[0, 1:2, :] = jnp.sum(grad_first * normal, axis=0, keepdims=True)
    gin_ref[...] = gmid_ref[...] + norm_back(grad_first, mod[1:2], normal, inverse)

def input_backward(patches, mod, gqkv, gmid, wqkv):
    tokens, width = patches.shape
    latents = mod.shape[0]
    seq = tokens // latents
    rows = lambda cols: pl.BlockSpec((seq, cols), lambda i: (i, 0))
    per = lambda a: pl.BlockSpec((1,) + a.shape[1:], lambda i: (i, 0, 0))
    whole = lambda a: pl.BlockSpec(a.shape, lambda i: (0, 0), pipeline_mode=pl.Buffered(1))
    return pl.pallas_call(
        input_backward_kernel, grid=(latents,),
        in_specs=[rows(width), per(mod), rows(3 * width), rows(width), whole(wqkv)],
        out_specs=[rows(width), pl.BlockSpec((1, 2, width), lambda i: (i, 0, 0))],
        out_shape=[jax.ShapeDtypeStruct((tokens, width), jnp.float32), jax.ShapeDtypeStruct((latents, 2, width), jnp.float32)],
        compiler_params=pltpu.CompilerParams(vmem_limit_bytes=VMEM_BYTES))(patches, mod, gqkv, gmid, wqkv)


def cost(flops, size):
    return pl.CostEstimate(flops=int(flops), bytes_accessed=int(size), transcendentals=0)


def feed_forward_step(x_ref, g_ref, up_ref, down_ref, act_ref, gpre_ref, out_acc, grad_acc):
    inner_scale = SQRT_TWO_OVER_PI
    cubic = 0.044715
    pre = nn(x_ref[...], up_ref[...])
    grad_act = nt(g_ref[...], down_ref[...])
    squared = pre * pre
    bent = jnp.tanh(pre * (inner_scale + (inner_scale * cubic) * squared))
    half = 0.5 + 0.5 * bent
    act = (pre * half).astype(jnp.bfloat16)
    slope = half + (0.5 * pre) * (1.0 - bent * bent) * (
        inner_scale + (3.0 * cubic * inner_scale) * squared
    )
    grad_pre = (grad_act * slope).astype(jnp.bfloat16)
    act_ref[...] = act
    gpre_ref[...] = grad_pre
    out_acc[...] += nn(act, down_ref[...])
    grad_acc[...] += nt(grad_pre, up_ref[...])


def shared_kernel(
    x_ref, cot_ref, gate_ref, up_ref, down_ref,
    act_ref, gpre_ref, g_ref, out_ref, grad_ref,
    out_acc, grad_acc,
):
    step = pl.program_id(0)
    latents = gate_ref.shape[0]
    seq = x_ref.shape[0] // latents

    @pl.when(step == 0)
    def _():
        out_acc[...] = jnp.zeros_like(out_acc)
        grad_acc[...] = jnp.zeros_like(grad_acc)
        for i in range(latents):
            rows = slice(i * seq, (i + 1) * seq)
            g_ref[rows, :] = (gate_ref[i : i + 1, :] * cot_ref[rows, :].astype(jnp.float32)).astype(
                jnp.bfloat16
            )

    feed_forward_step(x_ref, g_ref, up_ref, down_ref, act_ref, gpre_ref, out_acc, grad_acc)

    @pl.when(step == pl.num_programs(0) - 1)
    def _():
        out_ref[...] = out_acc[...]
        grad_ref[...] = grad_acc[...]


def tile_of(width):
    return width // 4 if width % 512 == 0 else width


def still(array):
    return pl.BlockSpec(
        array.shape, lambda j, n=len(array.shape): (0,) * n, pipeline_mode=pl.Buffered(1)
    )


def shared_forward_backward(x, cot, gate, up, down):
    rows, width = x.shape
    hidden = up.shape[1]
    tile = tile_of(hidden)
    out = jax.ShapeDtypeStruct((rows, width), jnp.float32)
    wide = jax.ShapeDtypeStruct((rows, hidden), jnp.bfloat16)
    fixed = pl.BlockSpec((rows, width), lambda j: (0, 0))
    column = pl.BlockSpec((rows, tile), lambda j: (0, j))
    return pl.pallas_call(
        shared_kernel,
        grid=(hidden // tile,),
        in_specs=[
            still(x), still(cot), still(gate),
            pl.BlockSpec((width, tile), lambda j: (0, j)),
            pl.BlockSpec((tile, width), lambda j: (j, 0)),
        ],
        out_specs=[column, column, fixed, fixed, fixed],
        out_shape=[wide, wide, jax.ShapeDtypeStruct((rows, width), jnp.bfloat16), out, out],
        scratch_shapes=[pltpu.VMEM((rows, width), jnp.float32)] * 2,
        compiler_params=pltpu.CompilerParams(vmem_limit_bytes=VMEM_BYTES),
        cost_estimate=cost(8 * rows * width * hidden, 4 * width * hidden + 4 * rows * hidden),
        name="shared_ffn",
    )(x, cot, gate, up, down)


def expert_kernel(blocks, carried, *refs):
    xs, cots = refs[:blocks], refs[blocks : 2 * blocks]
    slot_row, slot_col, gate_col, gate_two, up_ref, down_ref = refs[2 * blocks : 2 * blocks + 6]
    rest = refs[2 * blocks + 6 + carried :]
    act_ref, gpre_ref, x_ref, g_ref = rest[:4]
    mixes, backs = rest[4 : 4 + blocks], rest[4 + blocks : 4 + 2 * blocks]
    out_acc, grad_acc = rest[4 + 2 * blocks :]
    step = pl.program_id(0)
    tokens = xs[0].shape[0]
    capacity = x_ref.shape[0] // blocks
    latents = gate_two.shape[1]
    seq = tokens // latents

    @pl.when(step == 0)
    def _():
        out_acc[...] = jnp.zeros_like(out_acc)
        grad_acc[...] = jnp.zeros_like(grad_acc)
        for b in range(blocks):
            rows = slice(b * capacity, (b + 1) * capacity)
            places = lax.broadcasted_iota(jnp.int32, (capacity, tokens), 0)
            pick = (places == slot_row[b]).astype(jnp.float32).astype(jnp.bfloat16)
            x_ref[rows, :] = nn(pick, xs[b][...]).astype(jnp.bfloat16)
            grads = []
            for i in range(latents):
                part = slice(i * seq, (i + 1) * seq)
                branch = gate_two[b, i : i + 1, :] * cots[b][part, :].astype(jnp.float32)
                grads.append((gate_col[b, part, :] * branch).astype(jnp.bfloat16))
            grad = jnp.concatenate(grads, axis=0)
            g_ref[rows, :] = nn(pick, grad).astype(jnp.bfloat16)

    feed_forward_step(x_ref, g_ref, up_ref, down_ref, act_ref, gpre_ref, out_acc, grad_acc)

    @pl.when(step == pl.num_programs(0) - 1)
    def _():
        for b in range(blocks):
            rows = slice(b * capacity, (b + 1) * capacity)
            places = lax.broadcasted_iota(jnp.int32, (tokens, capacity), 1)
            pick = (places == slot_col[b]).astype(jnp.float32).astype(jnp.bfloat16)
            backs[b][...] = nn(pick, grad_acc[rows, :].astype(jnp.bfloat16)).astype(jnp.bfloat16)
            mixed = nn(pick, out_acc[rows, :].astype(jnp.bfloat16))
            mixes[b][...] = (gate_col[b] * mixed).astype(jnp.bfloat16)


def expert_forward_backward(
    xs, cots, slot_row, slot_col, gate_col, gate_two, up, down, capacity, groups, group, carried
):
    blocks = len(xs)
    tokens, width = xs[0].shape
    hidden = up.shape[1]
    tile = tile_of(hidden)
    rows = blocks * capacity
    total = rows * groups
    wide = jax.ShapeDtypeStruct((total, hidden), jnp.bfloat16)
    slim = jax.ShapeDtypeStruct((total, width), jnp.bfloat16)
    token = jax.ShapeDtypeStruct((tokens, width), jnp.bfloat16)
    column = pl.BlockSpec((rows, tile), lambda j: (group, j))
    own = pl.BlockSpec((rows, width), lambda j: (group, 0))
    fixed = pl.BlockSpec((tokens, width), lambda j: (0, 0))
    small = [slot_row, slot_col, gate_col, gate_two]
    first = 2 * blocks + 6
    return pl.pallas_call(
        functools.partial(expert_kernel, blocks, len(carried)),
        grid=(hidden // tile,),
        in_specs=[still(a) for a in (*xs, *cots, *small)]
        + [
            pl.BlockSpec((width, tile), lambda j: (0, j)),
            pl.BlockSpec((tile, width), lambda j: (j, 0)),
        ]
        + [pl.BlockSpec(memory_space=pl.ANY)] * len(carried),
        out_specs=[column, column, own, own] + [fixed] * (2 * blocks),
        out_shape=[wide, wide, slim, slim] + [token] * (2 * blocks),
        scratch_shapes=[pltpu.VMEM((rows, width), jnp.float32)] * 2,
        input_output_aliases={first + i: i for i in range(len(carried))},
        compiler_params=pltpu.CompilerParams(vmem_limit_bytes=VMEM_BYTES),
        cost_estimate=cost(8 * rows * width * hidden, 4 * width * hidden + 4 * rows * hidden),
        name="expert_ffn",
    )(*xs, *cots, *small, up, down, *carried)


def weight_grad_kernel(steps, along_columns, moves, table, a_ref, b_ref, *rest):
    count = len({m[0] for m in moves})
    outs = rest[:count]
    sum_ref, sems = rest[count], rest[count + 1]
    step = pl.program_id(0)
    if along_columns:
        turned = rest[count + 2]
        tile = b_ref.shape[1]

        @pl.when(step == 0)
        def _():
            turned[...] = a_ref[...].T

        sum_ref[:, pl.ds(pl.multiple_of(step * tile, tile), tile)] = nn(
            turned[...], b_ref[...]
        ).astype(jnp.bfloat16)
    else:
        tile = a_ref.shape[1]
        sum_ref[pl.ds(pl.multiple_of(step * tile, tile), tile), :] = tn(
            a_ref[...], b_ref[...]
        ).astype(jnp.bfloat16)

    @pl.when(step == steps - 1)
    def _():
        copies = []
        for i, (out, row, rows, row_from, col_from, cols) in enumerate(moves):
            entry, scale, offset = row_from
            start = table[entry] * scale + offset
            if isinstance(col_from, tuple):
                chooser, half, shift = col_from
                column = pl.multiple_of(table[chooser] * half + shift, 128)
            else:
                column = col_from
            copies.append(
                pltpu.make_async_copy(
                    sum_ref.at[pl.ds(pl.multiple_of(start, 8), rows), pl.ds(column, cols)],
                    outs[out].at[pl.ds(row, rows), :],
                    sems.at[i],
                )
            )
        for copy in copies:
            copy.start()
        for copy in copies:
            copy.wait()


def weight_grad(a, b, table, moves, shapes, name):
    rows, left = a.shape
    right = b.shape[1]
    along_columns = left < 1024
    if along_columns:
        tile = right // 3 if right // 3 % 128 == 0 and right > 1024 else right
        steps = right // tile
        specs = [
            pl.BlockSpec((rows, left), lambda j, t: (0, 0), pipeline_mode=pl.Buffered(1)),
            pl.BlockSpec((rows, tile), lambda j, t: (0, j)),
        ]
        extra = [pltpu.VMEM((left, rows), jnp.bfloat16)]
    else:
        tile = tile_of(left)
        steps = left // tile
        specs = [
            pl.BlockSpec((rows, tile), lambda j, t: (0, j)),
            pl.BlockSpec((rows, right), lambda j, t: (0, 0), pipeline_mode=pl.Buffered(1)),
        ]
        extra = []
    return pl.pallas_call(
        functools.partial(weight_grad_kernel, steps, along_columns, moves),
        grid_spec=pltpu.PrefetchScalarGridSpec(
            num_scalar_prefetch=1,
            grid=(steps,),
            in_specs=specs,
            out_specs=[pl.BlockSpec(memory_space=pl.ANY)] * len(shapes),
            scratch_shapes=[
                pltpu.VMEM((left, right), jnp.bfloat16),
                pltpu.SemaphoreType.DMA((len(moves),)),
                *extra,
            ],
        ),
        out_shape=[jax.ShapeDtypeStruct(s, jnp.bfloat16) for s in shapes],
        compiler_params=pltpu.CompilerParams(vmem_limit_bytes=VMEM_BYTES),
        cost_estimate=cost(2 * rows * left * right, 2 * left * right + 2 * rows * (left + right)),
        name=name,
    )(table, a, b)


def bits_of(size):
    return size.bit_length() - 1


def label_of(index):
    upper = index >> 1
    return ((upper ^ (upper >> 1)) << 1) | (index & 1)


def index_of(label):
    upper = label >> 1
    shift = 1
    while shift < 32:
        upper = upper ^ (upper >> shift)
        shift *= 2
    return (upper << 1) | (label & 1)


def swap_dp(value, bit):
    size = lax.axis_size("dp")
    return lax.ppermute(
        value, "dp", [(i, index_of(label_of(i) ^ (1 << bit))) for i in range(size)]
    )


def swap_expert(value, bit):
    size = lax.axis_size("expert")
    return lax.ppermute(value, "expert", [(i, i ^ (1 << bit)) for i in range(size)])


def gather_expert(value):
    bits = bits_of(lax.axis_size("expert"))
    parts = {0: value}
    for bit in reversed(range(bits)):
        for r in list(parts):
            parts[r | (1 << bit)] = swap_expert(parts[r], bit)
    return [parts[r] for r in range(1 << bits)]


def gather_ordered(value):
    mine = lax.axis_index("expert")
    for bit in range(bits_of(lax.axis_size("expert"))):
        other = swap_expert(value, bit)
        upper = (mine >> bit & 1) == 1
        value = jnp.concatenate(
            [jnp.where(upper, other, value), jnp.where(upper, value, other)], axis=0
        )
    return value


def scatter_expert(parts):
    parts = [[part] for part in parts]
    for bit in range(bits_of(lax.axis_size("expert"))):
        left = []
        for kept, away in zip(parts[::2], parts[1::2]):
            away = away[0] if len(away) == 1 else added(away).astype(jnp.bfloat16)
            kept = kept if len(kept) == 1 else [added(kept).astype(jnp.bfloat16)]
            left.append([*kept, swap_expert(away, bit)])
        parts = left
    return parts[0]


def gather_dp(value):
    for bit in range(bits_of(lax.axis_size("dp"))):
        value = jnp.concatenate([value, swap_dp(value, bit)], axis=0)
    return value


def orders(size):
    bits = bits_of(size)
    return [[(start + step) % bits for step in range(bits)] for start in range(PARTS)]


def shard_table(size):
    places = np.zeros((PARTS, size), np.int32)
    for part, order in enumerate(orders(size)):
        for place in range(size):
            for step, bit in enumerate(order):
                if place >> (len(order) - 1 - step) & 1:
                    places[part, place] |= 1 << bit
    owners = index_of(label_of(lax.axis_index("dp")) ^ jnp.asarray(places.reshape(-1)))
    core = lax.axis_index("expert") & 1
    return jnp.concatenate([owners, core[None], 1 - core[None]]).astype(jnp.int32)


def pieces_moves(size, left, right, by_rows):
    shard = left // size
    moves = []
    for part in range(PARTS):
        for place in range(size):
            out = 2 * part + (place >= size // 2)
            at = place % (size // 2)
            entry = part * size + place
            if by_rows:
                rows = shard // PARTS
                moves.append((out, at * rows, rows, (entry, shard, part * rows), 0, right))
            else:
                cols = right // PARTS
                moves.append((out, at * shard, shard, (entry, shard, 0), part * cols, cols))
    if by_rows:
        shape = (left // 2 // PARTS, right)
    else:
        shape = (left // 2, right // PARTS)
    return moves, [shape] * (2 * PARTS)


def dense_moves(size, left, right):
    shard = left // size
    half = right // 2
    cols = half // PARTS
    moves = []
    for out in range(2):
        for part in range(PARTS):
            for place in range(size):
                entry = part * size + place
                chooser = PARTS * size + (1 - out)
                moves.append(
                    (
                        out, part * left + place * shard, shard,
                        (entry, shard, 0), (chooser, half, part * cols), cols,
                    )
                )
    return moves, [(PARTS * left, cols)] * 2


def added(parts):
    total = parts[0].astype(jnp.float32)
    for part in parts[1:]:
        total = total + part.astype(jnp.float32)
    return total


def sum_over_dp(away, kept, order):
    for step, bit in enumerate(order):
        kept = [*kept, swap_dp(away, bit)]
        half = kept[0].shape[0] // 2
        if step + 1 < len(order):
            away = added([k[half:] for k in kept]).astype(jnp.bfloat16)
            kept = [k[:half] for k in kept]
    return added(kept)


def sum_pieces(pieces, size, by_rows):
    sums = [
        sum_over_dp(pieces[2 * part + 1], [pieces[2 * part]], order)
        for part, order in enumerate(orders(size))
    ]
    return jnp.concatenate(sums, axis=0 if by_rows else 1)


def sum_dense(away, mine, size):
    kept = [mine, swap_expert(away, 0)]
    left = mine.shape[0] // PARTS
    sums = []
    for part, order in enumerate(orders(size)):
        low = [k[part * left : part * left + left // 2] for k in kept]
        high = [k[part * left + left // 2 : (part + 1) * left] for k in kept]
        sums.append(sum_over_dp(added(high).astype(jnp.bfloat16), low, order))
    total = jnp.concatenate(sums, axis=1).astype(jnp.bfloat16)
    for bit in range(1, bits_of(lax.axis_size("expert"))):
        total = added([total, swap_expert(total, bit)]).astype(jnp.bfloat16)
    opposite = swap_expert(total, 0)
    upper = (lax.axis_index("expert") & 1) == 1
    return jnp.concatenate(
        [jnp.where(upper, opposite, total), jnp.where(upper, total, opposite)], axis=1
    ).astype(jnp.float32)


def on_device(
    patches,
    time_embed,
    ada_weight,
    ada_bias,
    qkv_weight,
    out_weight,
    up_weight,
    down_weight,
    expert_up,
    expert_down,
    routes,
    gate_weights,
    cotangent,
):
    tokens, width = patches.shape
    latents = time_embed.shape[0]
    seq_len = tokens // latents
    experts = lax.axis_size("expert")
    dp_size = lax.axis_size("dp")
    dp_index = lax.axis_index("dp")
    expert_index = lax.axis_index("expert")
    capacity = 5 * tokens // (2 * experts)
    table = shard_table(dp_size)

    cond = jax.nn.silu(time_embed.astype(jnp.float32)).astype(jnp.bfloat16)
    modulation = jnp.dot(cond, ada_weight, preferred_element_type=jnp.float32) + ada_bias
    mod = modulation.reshape(latents, 6, width)

    cots = gather_expert(cotangent)
    routes_all = jnp.stack(gather_expert(routes.T))
    gates_all = jnp.stack(gather_expert(gate_weights.T))
    time_group = jnp.concatenate(gather_expert(time_embed))
    time_all = gather_dp(gather_ordered(time_embed))

    cond_group = jax.nn.silu(time_group.astype(jnp.float32)).astype(jnp.bfloat16)
    gate_two_group = (
        jnp.dot(cond_group, ada_weight[:, 5 * width :], preferred_element_type=jnp.float32)
        + ada_bias[5 * width :]
    ).reshape(experts, latents, width)
    named = routes_all == expert_index
    member = jnp.any(named, axis=1)
    gate_here = jnp.sum(jnp.where(named, gates_all, 0.0), axis=1)
    position = jnp.arange(tokens, dtype=jnp.int32)
    before = (position[:, None] < position[None, :]).astype(jnp.bfloat16)
    slot = jnp.dot(
        member.astype(jnp.bfloat16), before, preferred_element_type=jnp.float32
    ).astype(jnp.int32)
    slot = jnp.where(member, slot, capacity)
    local_counts = jnp.sum(
        (routes[:, :, None] == jnp.arange(experts, dtype=jnp.int32)).astype(jnp.int32),
        axis=(0, 1),
    )
    slot_row, slot_col, gate_col = slot[:, None, :], slot[:, :, None], gate_here[:, :, None]

    first_in, qkv_all, log_total, attended, attn_proj, second_in = attn_forward(
        patches, mod, qkv_weight, out_weight
    )
    seconds = gather_expert(second_in)

    shared_act, grad_shared_pre, grad_shared, shared_out, grad_second = shared_forward_backward(
        second_in, cotangent, mod[:, 5], up_weight, down_weight
    )

    group_size = 2
    groups = experts // group_size
    carried = []
    mixes, backs = [], []
    for group in range(groups):
        span = slice(group * group_size, (group + 1) * group_size)
        results = expert_forward_backward(
            seconds[span], cots[span], slot_row[span], slot_col[span], gate_col[span],
            gate_two_group[span], expert_up[0], expert_down[0], capacity, groups, group, carried,
        )
        carried = results[:4]
        mixes += results[4 : 4 + group_size]
        backs += results[4 + group_size :]
    act_rows, grad_pre_rows, rows_in, grad_rows = carried
    back_kept, back_came = scatter_expert(backs)
    mix_kept, mix_came = scatter_expert(mixes)

    moves, shapes = pieces_moves(dp_size, act_rows.shape[1], width, True)
    down_pieces = weight_grad(act_rows, grad_rows, table, moves, shapes, "grad_expert_down")
    sum_e_down = sum_pieces(down_pieces, dp_size, True)
    moves, shapes = pieces_moves(dp_size, width, act_rows.shape[1], False)
    up_pieces = weight_grad(rows_in, grad_pre_rows, table, moves, shapes, "grad_expert_up")
    sum_e_up = sum_pieces(up_pieces, dp_size, False)

    moves, shapes = dense_moves(dp_size, shared_act.shape[1], width)
    sum_w_down = sum_dense(
        *weight_grad(shared_act, grad_shared, table, moves, shapes, "grad_down"), dp_size
    )
    moves, shapes = dense_moves(dp_size, width, shared_act.shape[1])
    sum_w_up = sum_dense(
        *weight_grad(second_in, grad_shared_pre, table, moves, shapes, "grad_up"), dp_size
    )

    grad_qkv_rows, grad_attn, grad_middle, grad_mod_early = attn_backward(
        patches, mod, attn_proj, qkv_all, log_total, cotangent, out_weight,
        [grad_second, back_kept, back_came],
    )
    moves, shapes = dense_moves(dp_size, width, 3 * width)
    sum_w_qkv = sum_dense(
        *weight_grad(first_in, grad_qkv_rows, table, moves, shapes, "grad_qkv"), dp_size
    )
    moves, shapes = dense_moves(dp_size, width, width)
    sum_w_out = sum_dense(
        *weight_grad(attended, grad_attn, table, moves, shapes, "grad_out"), dp_size
    )
    grad_input, grad_mod_late = input_backward(
        patches, mod, grad_qkv_rows, grad_middle, qkv_weight
    )

    middle = patches.astype(jnp.float32).reshape(latents, seq_len, width) + mod[
        :, 2:3
    ] * attn_proj.reshape(latents, seq_len, width)
    branch = (shared_out + added([mix_kept, mix_came])).reshape(latents, seq_len, width)
    block_out = (middle + mod[:, 5:6] * branch).reshape(tokens, width).astype(jnp.bfloat16)
    grad_gate_two = jnp.sum(
        cotangent.astype(jnp.float32).reshape(latents, seq_len, width) * branch, axis=1
    )

    count_parts = jnp.concatenate([local_counts // 128, local_counts % 128]).astype(jnp.bfloat16)
    count_rows = jnp.zeros((latents, 128), jnp.bfloat16).at[0, : 2 * experts].set(count_parts)
    early = jnp.concatenate(
        [
            grad_mod_early.reshape(latents, 3 * width).astype(jnp.bfloat16),
            grad_gate_two.astype(jnp.bfloat16),
            count_rows,
        ],
        axis=1,
    )
    late = grad_mod_late.reshape(latents, 2 * width).astype(jnp.bfloat16)
    early_all = gather_dp(gather_ordered(early))
    late_all = gather_dp(gather_ordered(late))
    grad_mod_all = jnp.concatenate([late_all, early_all[:, : 4 * width]], axis=1)
    count_sums = jnp.sum(early_all[:, 4 * width :].astype(jnp.float32), axis=0).astype(jnp.int32)
    counts = count_sums[:experts] * 128 + count_sums[experts : 2 * experts]
    cond_all = jax.nn.silu(time_all.astype(jnp.float32)).astype(jnp.bfloat16)
    ada_rows = width // dp_size
    cond_mine = lax.dynamic_slice_in_dim(cond_all.T, dp_index * ada_rows, ada_rows, axis=0)
    sum_ada = jnp.dot(cond_mine, grad_mod_all, preferred_element_type=jnp.float32)
    bias_all = jnp.sum(grad_mod_all.astype(jnp.float32), axis=0)
    bias_size = bias_all.shape[0] // dp_size
    sum_bias = lax.dynamic_slice_in_dim(bias_all, dp_index * bias_size, bias_size)
    return (
        block_out,
        grad_input,
        sum_ada,
        sum_bias,
        sum_w_qkv,
        sum_w_out,
        sum_w_up,
        sum_w_down,
        sum_e_up[None],
        sum_e_down[None],
        counts,
    )


def solution(mesh):
    in_specs = (
        P(("dp", "expert"), None),
        P(("dp", "expert"), None),
        P(),
        P(),
        P(),
        P(),
        P(),
        P(),
        P("expert", None, None),
        P("expert", None, None),
        P(("dp", "expert"), None),
        P(("dp", "expert"), None),
        P(("dp", "expert"), None),
    )
    out_specs = (
        P(("dp", "expert"), None),
        P(("dp", "expert"), None),
        P("dp", None),
        P("dp"),
        P("dp", None),
        P("dp", None),
        P("dp", None),
        P("dp", None),
        P("expert", "dp", None),
        P("expert", "dp", None),
        P(),
    )
    return jax.shard_map(
        on_device, mesh=mesh, in_specs=in_specs, out_specs=out_specs, check_vma=False
    )
```

time: 561 us -> 549 us (0.979)
  the two profiles are of different devices: /device:TPU:8 before, /device:TPU:0 now
where the time goes in v2:
time: 549 us; the launch traced here: 540 us
  waiting for transfers between devices  192 us (35%)
  Pallas kernels  153 us (28%)
  starting transfers between devices  137 us (25%)
  other arithmetic  34.2 us (6%)
  local copies, waits for them, and re-layouts  13.8 us (3%)
  matrix products  8.37 us (2%)
    ppermute x63, waiting for transfers between devices, swap_dp(): lax.ppermute(value, 'dp', [(i, index_of(label_of(i) ^ 1 << bit)) for i in...  141 us
    ppermute x63, starting transfers between devices, swap_dp(): lax.ppermute(value, 'dp', [(i, index_of(label_of(i) ^ 1 << bit)) for i in...  121 us
    pallas_call x6, Pallas kernels, weight_grad(): pl.pallas_call(functools.partial(weight_grad_kernel, steps, along_columns...  53.5 us
    ppermute x38, waiting for transfers between devices, swap_expert(): lax.ppermute(value, 'expert', [(i, i ^ 1 << bit) for i in range(size)])  51.3 us
    pallas_call x2, Pallas kernels, expert_forward_backward(): pl.pallas_call(functools.partial(expert_kernel, blocks, len(carried)), gr...  47 us
    pallas_call x1, Pallas kernels, shared_forward_backward(): pl.pallas_call(shared_kernel, grid=(hidden // tile,), in_specs=[still(x),...  16.4 us
    ppermute x38, starting transfers between devices, swap_expert(): lax.ppermute(value, 'expert', [(i, i ^ 1 << bit) for i in range(size)])  16 us
    pallas_call x1, Pallas kernels, attn_forward(): pl.pallas_call(attn_forward_kernel, grid=(latents,), in_specs=[rows(width...  15 us
  transfers between devices with their start and end apart: 101, of which 35 were waited for; matrix products, arithmetic and copies ran while one was open for 9% of the time, Pallas kernels for 28%

profile of v2, /device:TPU:0, one launch (start us, length us, event | category | flops | bytes accessed | tf_op | source)
XLA Modules:
  0.0 539.7 jit_solution(17929290687745979578)
XLA Ops:
  6.8 4.0 convolution_add_fusion
  12.7 15.0 %shard_map.221 = (bf16[512,768]{1,0:T(8,128)(2,1)}, bf16[512,2304]{1,0:T(8,128)(2,1)}, f32[2,12,256]{2,1,0:T(8,128)}, bf16[512,768]{1,0:T(8,128)(2,1)}, f32[512,768]{1,0:T(8,128)}, /*index=5*/bf16[512,768]{1,0:T(8,128)(2,1)}) custom-call(bf16[512,768]{1,0:T(8,128)(2,1)} %x_ref.5, f32[2,6,768]{2,1,0:T(8,128)} %reshape.95.mod_ref, bf16[768,2304]{1,0:T(8,128)(2,1)} %wqkv_ref.3, ...), custom_call_target="tpu_custom_call" | custom-call | tf_op jit(solution)/shard_map/pallas_call | solution.py:76
  27.7 16.4 %shared_ffn.1 = (bf16[512,3072]{1,0:T(8,128)(2,1)}, bf16[512,3072]{1,0:T(8,128)(2,1)}, bf16[512,768]{1,0:T(8,128)(2,1)}, f32[512,768]{1,0:T(8,128)}, f32[512,768]{1,0:T(8,128)}) custom-call(bf16[512,768]{1,0:T(8,128)(2,1)} %get-tuple-element.77.x_ref.refs_0_.a_ref, bf16[512,768]{1,0:T(8,128)(2,1)} %cot_ref.3, f32[2,768]{1,0:T(2,128)} %slice_bitcast_fusion.gate_ref, ...), custom_call_target="tpu_custom_call" | custom-call | flops 9663676416 | bytes 15728640 | tf_op jit(solution)/shard_map/shared_ffn/pallas_call | solution.py:234
  44.1 8.2 %grad_up.1 = (bf16[2304,512]{1,0:T(8,128)(2,1)}, bf16[2304,512]{1,0:T(8,128)(2,1)}) custom-call(s32[26]{0:T(128)} %pad_add_fusion.table, bf16[512,768]{1,0:T(8,128)(2,1)} %get-tuple-element.77.x_ref.refs_0_.a_ref, bf16[512,3072]{1,0:T(8,128)(2,1)} %get-tuple-element.106.b_ref), custom_call_target="tpu_custom_call" | custom-call | flops 2415919104 | bytes 8650752 | tf_op jit(solution)/shard_map/grad_up/pallas_call | solution.py:396
  52.4 8.5 %grad_down.1 = (bf16[9216,128]{1,0:T(8,128)(2,1)}, bf16[9216,128]{1,0:T(8,128)(2,1)}) custom-call(s32[26]{0:T(128)} %pad_add_fusion.table, bf16[512,3072]{1,0:T(8,128)(2,1)} %get-tuple-element.109.a_ref, bf16[512,768]{1,0:T(8,128)(2,1)} %get-tuple-element.110.b_ref), custom_call_target="tpu_custom_call" | custom-call | flops 2415919104 | bytes 8650752 | tf_op jit(solution)/shard_map/grad_down/pallas_call | solution.py:396
  69.6 34.6 %collective-permute-done.21 = bf16[4,768]{1,0:T(4,128)(2,1)S(1)} collective-permute-done((bf16[4,768]{1,0:T(4,128)(2,1)S(1)}, bf16[4,768]{1,0:T(4,128)(2,1)S(1)}, u32[]{:S(2)}, u32[]{:S(2)}) %collective-permute-start.21) | collective-permute-done | bytes 6176 | tf_op jit(solution)/shard_map/ppermute | solution.py:443
  122.7 23.7 %expert_ffn.2 = (bf16[1280,3072]{1,0:T(8,128)(2,1)}, bf16[1280,3072]{1,0:T(8,128)(2,1)}, bf16[1280,768]{1,0:T(8,128)(2,1)}, bf16[1280,768]{1,0:T(8,128)(2,1)}, b...) custom-call(bf16[512,768]{1,0:T(8,128)(2,1)} %get-tuple-element.77.x_re, ...), custom_call_target="tpu_custom_call" | custom-call | flops 12079595520 | bytes 17301504 | tf_op jit(solution)/shard_map/expert_ffn/pallas_call | solution.py:311
  147.6 23.3 %expert_ffn.3 = (bf16[1280,3072]{1,0:T(8,128)(2,1)}, bf16[1280,3072]{1,0:T(8,128)(2,1)}, bf16[1280,768]{1,0:T(8,128)(2,1)}, bf16[1280,768]{1,0:T(8,128)(2,1)}, b...) custom-call(bf16[512,768]{1,0:T(8,128)(2,1)} %collective-permute-don, ...), custom_call_target="tpu_custom_call", output_to_operand_aliasing={{0}: (10, {}), {1}: (11, {}), {2}: (12, {}), {3}: (13, {})} | custom-call | flops 12079595520 | bytes 17301504 | tf_op jit(solution)/shard_map/expert_ffn/pallas_call | solution.py:311
  170.9 12.3 %grad_expert_down.1 = (bf16[512,768]{1,0:T(8,128)(2,1)}, bf16[512,768]{1,0:T(8,128)(2,1)}, bf16[512,768]{1,0:T(8,128)(2,1)}, bf16[512,768]{1,0:T(8,128)(2,1)}, b...) custom-call(s32[26]{0:T(128)} %pad_add_fusion.table, bf16[1280,3072]{1,0:T(8,128)(2,1)} %get-tuple-element.121.a_ref, ...), custom_call_target="tpu_custom_call" | custom-call | flops 6039797760 | bytes 14548992 | tf_op jit(solution)/shard_map/grad_expert_down/pallas_call | solution.py:396
  184.8 12.7 %grad_expert_up.1 = (bf16[384,1024]{1,0:T(8,128)(2,1)}, bf16[384,1024]{1,0:T(8,128)(2,1)}, bf16[384,1024]{1,0:T(8,128)(2,1)}, bf16[384,1024]{1,0:T(8,128)(2,1)},...) custom-call(s32[26]{0:T(128)} %pad_add_fusion.table, bf16[1280,768]{1,0:T(8,128)(2,1)} %get-tuple-element.113.a_ref, ...), custom_call_target="tpu_custom_call" | custom-call | flops 6039797760 | bytes 14548992 | tf_op jit(solution)/shard_map/grad_expert_up/pallas_call | solution.py:396
  203.7 18.4 %collective-permute-done.95 = bf16[512,768]{1,0:T(8,128)(2,1)S(1)} collective-permute-done((bf16[512,768]{1,0:T(8,128)(2,1)}, bf16[512,768]{1,0:T(8,128)(2,1)S(1)}, u32[]{:S(2)}, u32[]{:S(2)}) %collective-permute-start.95) | collective-permute-done | bytes 786464 | tf_op jit(solution)/shard_map/ppermute | solution.py:436
  222.7 15.9 %collective-permute-start.93 = (bf16[256,768]{1,0:T(8,128)(2,1)S(1)}, bf16[256,768]{1,0:T(8,128)(2,1)S(1)}, u32[]{:S(2)}, u32[]{:S(2)}) collective-permute-start(bf16[256,768]{1,0:T(8,128)(2,1)S(1)} %add_convert_fusion.6), channel_id=1, source_target_pairs={{0,8},{4,12},{8,0},{12,4},{16,24},{20,28},{24,16},{28,20},{1,9},{5... | collective-permute-start | bytes 1179656 | tf_op jit(solution)/shard_map/ppermute | solution.py:436
  240.8 15.1 %collective-permute-done.86 = bf16[384,1024]{1,0:T(8,128)(2,1)S(1)} collective-permute-done((bf16[384,1024]{1,0:T(8,128)(2,1)S(1)}, bf16[384,1024]{1,0:T(8,128)(2,1)S(1)}, u32[]{:S(2)}, u32[]{:S(2)}) %collective-permute-start.86) | collective-permute-done | bytes 786464 | tf_op jit(solution)/shard_map/ppermute | solution.py:436
  256.0 3.9 collective-permute-start.96
  260.6 28.8 %collective-permute-done.75 = bf16[1536,128]{1,0:T(8,128)(2,1)S(1)} collective-permute-done((bf16[1536,128]{1,0:T(8,128)(2,1)S(1)}, bf16[1536,128]{1,0:T(8,128)(2,1)S(1)}, u32[]{:S(2)}, u32[]{:S(2)}) %collective-permute-start.75) | collective-permute-done | bytes 393248 | tf_op jit(solution)/shard_map/ppermute | solution.py:436
  293.4 21.2 %collective-permute-start.63 = (bf16[384,512]{1,0:T(8,128)(2,1)S(1)}, bf16[384,512]{1,0:T(8,128)(2,1)S(1)}, u32[]{:S(2)}, u32[]{:S(2)}) collective-permute-start(bf16[384,512]{1,0:T(8,128)(2,1)S(1)} %get-tuple-element.150), channel_id=1, source_target_pairs={{0,8},{4,12},{8,0},{12,4},{16,24},{20,28},{24,16},{28,20},{1,9},{5... | collective-permute-start | bytes 1179656 | tf_op jit(solution)/shard_map/ppermute | solution.py:436
  319.5 4.8 collective-permute-done.63
  325.7 8.5 %collective-permute-done.66 = bf16[384,512]{1,0:T(8,128)(2,1)S(1)} collective-permute-done((bf16[384,512]{1,0:T(8,128)(2,1)S(1)}, bf16[384,512]{1,0:T(8,128)(2,1)S(1)}, u32[]{:S(2)}, u32[]{:S(2)}) %collective-permute-start.66) | collective-permute-done | bytes 393248 | tf_op jit(solution)/shard_map/ppermute | solution.py:436
  334.3 9.2 %collective-permute-start.100 = (bf16[128,768]{1,0:T(8,128)(2,1)S(1)}, bf16[128,768]{1,0:T(8,128)(2,1)S(1)}, u32[]{:S(2)}, u32[]{:S(2)}) collective-permute-start(bf16[128,768]{1,0:T(8,128)(2,1)S(1)} %add_convert_fusion.22), channel_id=1, source_target_pairs={{0,8},{4,12},{8,0},{12,4},{16,24},{20,28},{24,16},{28,20},{1,9},{5... | collective-permute-start | bytes 589832 | tf_op jit(solution)/shard_map/ppermute | solution.py:436
  344.9 8.4 %collective-permute-done.85 = bf16[96,1024]{1,0:T(8,128)(2,1)S(1)} collective-permute-done((bf16[96,1024]{1,0:T(8,128)(2,1)S(1)}, bf16[96,1024]{1,0:T(8,128)(2,1)S(1)}, u32[]{:S(2)}, u32[]{:S(2)}) %collective-permute-start.85) | collective-permute-done | bytes 196640 | tf_op jit(solution)/shard_map/ppermute | solution.py:436
  354.0 5.0 collective-permute-done.88
  376.0 5.6 %collective-permute-done.61 = bf16[192,512]{1,0:T(8,128)(2,1)S(1)} collective-permute-done((bf16[192,512]{1,0:T(8,128)(2,1)S(1)}, bf16[192,512]{1,0:T(8,128)(2,1)S(1)}, u32[]{:S(2)}, u32[]{:S(2)}) %collective-permute-start.61) | collective-permute-done | bytes 196640 | tf_op jit(solution)/shard_map/ppermute | solution.py:436
  399.6 14.2 %shard_map.222 = (bf16[512,2304]{1,0:T(8,128)(2,1)}, bf16[512,768]{1,0:T(8,128)(2,1)}, f32[512,768]{1,0:T(8,128)}, f32[2,3,768]{2,1,0:T(4,128)}) custom-call(bf16[512,768]{1,0:T(8,128)(2,1)} %x_ref.5, f32[2,6,768]{2,1,0:T(8,128)} %reshape.95.mod_ref, f32[512,768]{1,0:T(8,128)} %get-tuple-element.76.proj_ref, bf16[512,2304]{1,0:T(8,128)(2,1)} %get-tuple-element.87.qkv_ref, ...), custom_call_target="tpu_custom_call" | custom-call | tf_op jit(solution)/shard_map/pallas_call | solution.py:135
  413.8 6.5 %shard_map.223 = (f32[512,768]{1,0:T(8,128)}, f32[2,2,768]{2,1,0:T(2,128)}) custom-call(bf16[512,768]{1,0:T(8,128)(2,1)} %x_ref.5, f32[2,6,768]{2,1,0:T(8,128)} %reshape.95.mod_ref, bf16[512,2304]{1,0:T(8,128)(2,1)} %get-tuple-element.94.gqkv_ref.b_ref, f32[512,768]{1,0:T(8,128)} %get-tuple-element.95.gmid_ref, bf16[768,2304]{1,0:T(8,128)(2,1)} %wqkv_ref.3), custom_call_target="tpu_custom_call" | custom-call | tf_op jit(solution)/shard_map/pallas_call | solution.py:158
  421.2 4.3 grad_out.1
  429.0 7.5 %grad_qkv.1 = (bf16[2304,384]{1,0:T(8,128)(2,1)}, bf16[2304,384]{1,0:T(8,128)(2,1)}) custom-call(s32[26]{0:T(128)} %pad_add_fusion.table, bf16[512,768]{1,0:T(8,128)(2,1)} %get-tuple-element.99.a_ref, bf16[512,2304]{1,0:T(8,128)(2,1)} %get-tuple-element.94.gqkv_ref.b_ref), custom_call_target="tpu_custom_call" | custom-call | flops 1811939328 | bytes 6684672 | tf_op jit(solution)/shard_map/grad_qkv/pallas_call | solution.py:396
  443.4 6.0 %collective-permute-done.26 = bf16[4,1536]{1,0:T(4,128)(2,1)S(1)} collective-permute-done((bf16[4,1536]{1,0:T(4,128)(2,1)S(1)}, bf16[4,1536]{1,0:T(4,128)(2,1)S(1)}, u32[]{:S(2)}, u32[]{:S(2)}) %collective-permute-start.26) | collective-permute-done | bytes 12320 | tf_op jit(solution)/shard_map/ppermute | solution.py:443
  458.6 5.5 %collective-permute-done.29 = bf16[32,1536]{1,0:T(8,128)(2,1)S(1)} collective-permute-done((bf16[32,1536]{1,0:T(8,128)(2,1)S(1)}, bf16[32,1536]{1,0:T(8,128)(2,1)S(1)}, u32[]{:S(2)}, u32[]{:S(2)}) %collective-permute-start.29) | collective-permute-done | bytes 98336 | tf_op jit(solution)/shard_map/ppermute | solution.py:436
  466.9 3.9 collective-permute-done.69
  500.7 7.1 %collective-permute-done.42 = bf16[384,384]{1,0:T(8,128)(2,1)S(1)} collective-permute-done((bf16[384,384]{1,0:T(8,128)(2,1)S(1)}, bf16[384,384]{1,0:T(8,128)(2,1)S(1)}, u32[]{:S(2)}, u32[]{:S(2)}) %collective-permute-start.42) | collective-permute-done | bytes 294944 | tf_op jit(solution)/shard_map/ppermute | solution.py:436
  519.0 4.0 collective-permute-done.38
  530.8 5.8 %collective-permute-done.45 = bf16[96,1152]{1,0:T(8,128)(2,1)S(1)} collective-permute-done((bf16[96,1152]{1,0:T(8,128)(2,1)S(1)}, bf16[96,1152]{1,0:T(8,128)(2,1)S(1)}, u32[]{:S(2)}, u32[]{:S(2)}) %collective-permute-start.45) | collective-permute-done | bytes 221216 | tf_op jit(solution)/shard_map/ppermute | solution.py:443
  (401 shorter events, 168.9 us)
Async XLA Ops:
  0.6 62.4 %collective-permute-start.6 = (f32[2,512]{1,0:T(2,128)}, f32[2,512]{1,0:T(2,128)S(1)}, u32[]{:S(2)}, u32[]{:S(2)}) collective-permute-start(f32[2,512]{1,0:T(2,128)} %bitcast.70), channel_id=1, source_target_pairs={{0,2},{1,3},{2,0},{3,1},{4,6},{5,7},{6,4},{7,5},{8,10},{9,11},{10,... | collective-permute-start | bytes 12296 | tf_op jit(solution)/shard_map/ppermute | solution.py:443
  3.7 63.4 %collective-permute-start.5 = (f32[2,512]{1,0:T(2,128)}, f32[2,512]{1,0:T(2,128)S(1)}, u32[]{:S(2)}, u32[]{:S(2)}) collective-permute-start(f32[2,512]{1,0:T(2,128)} %bitcast.71), channel_id=1, source_target_pairs={{0,1},{1,0},{2,3},{3,2},{4,5},{5,4},{6,7},{7,6},{8,9},{9,8},{10,11... | collective-permute-start | bytes 12296 | tf_op jit(solution)/shard_map/ppermute | solution.py:443
  3.7 58.8 %collective-permute-start.9 = (bf16[2,768]{1,0:T(2,128)(2,1)}, bf16[2,768]{1,0:T(2,128)(2,1)S(1)}, u32[]{:S(2)}, u32[]{:S(2)}) collective-permute-start(bf16[2,768]{1,0:T(2,128)(2,1)} %param.17), channel_id=1, source_target_pairs={{0,2},{1,3},{2,0},{3,1},{4,6},{5,7},{6,4},{7,5},{8,10},{9,11},{10,... | collective-permute-start | bytes 9224 | tf_op jit(solution)/shard_map/ppermute | solution.py:443
  3.8 58.7 %collective-permute-start.8 = (bf16[2,768]{1,0:T(2,128)(2,1)}, bf16[2,768]{1,0:T(2,128)(2,1)S(1)}, u32[]{:S(2)}, u32[]{:S(2)}) collective-permute-start(bf16[2,768]{1,0:T(2,128)(2,1)} %param.17), channel_id=1, source_target_pairs={{0,1},{1,0},{2,3},{3,2},{4,5},{5,4},{6,7},{7,6},{8,9},{9,8},{10,11... | collective-permute-start | bytes 9224 | tf_op jit(solution)/shard_map/ppermute | solution.py:443
  4.2 59.1 %collective-permute-start.3 = (s32[2,512]{1,0:T(2,128)}, s32[2,512]{1,0:T(2,128)S(1)}, u32[]{:S(2)}, u32[]{:S(2)}) collective-permute-start(s32[2,512]{1,0:T(2,128)} %bitcast.67), channel_id=1, source_target_pairs={{0,2},{1,3},{2,0},{3,1},{4,6},{5,7},{6,4},{7,5},{8,10},{9,11},{10,... | collective-permute-start | bytes 12296 | tf_op jit(solution)/shard_map/ppermute | solution.py:443
  63.1 58.6 %collective-permute-start = (bf16[512,768]{1,0:T(8,128)(2,1)}, bf16[512,768]{1,0:T(8,128)(2,1)}, u32[]{:S(2)}, u32[]{:S(2)}) collective-permute-start(bf16[512,768]{1,0:T(8,128)(2,1)} %get-tuple-element.77.x_ref.refs_0_.a_ref), channel_id=1, source_target_pairs={{0,1},{1,0},{2,3},{3,2},{4,5},{5,4},{6,7},{7,6},{8,9},{9,8},{10,11... | collective-permute-start | bytes 2359304 | tf_op jit(solution)/shard_map/ppermute | solution.py:443
  67.0 55.7 %collective-permute-start.1 = (bf16[512,768]{1,0:T(8,128)(2,1)S(1)}, bf16[512,768]{1,0:T(8,128)(2,1)}, u32[]{:S(2)}, u32[]{:S(2)}) collective-permute-start(bf16[512,768]{1,0:T(8,128)(2,1)S(1)} %copy-done.3), channel_id=1, source_target_pairs={{0,1},{1,0},{2,3},{3,2},{4,5},{5,4},{6,7},{7,6},{8,9},{9,8},{10,11... | collective-permute-start | bytes 2359304 | tf_op jit(solution)/shard_map/ppermute | solution.py:443
  67.2 55.0 %collective-permute-start.12 = (bf16[512,768]{1,0:T(8,128)(2,1)}, bf16[512,768]{1,0:T(8,128)(2,1)}, u32[]{:S(2)}, u32[]{:S(2)}) collective-permute-start(bf16[512,768]{1,0:T(8,128)(2,1)} %get-tuple-element.77.x_ref.refs_0_.a_ref), channel_id=1, source_target_pairs={{0,2},{1,3},{2,0},{3,1},{4,6},{5,7},{6,4},{7,5},{8,10},{9,11},{10,... | collective-permute-start | bytes 2359304 | tf_op jit(solution)/shard_map/ppermute | solution.py:443
  67.5 54.7 %collective-permute-start.14 = (bf16[512,768]{1,0:T(8,128)(2,1)S(1)}, bf16[512,768]{1,0:T(8,128)(2,1)}, u32[]{:S(2)}, u32[]{:S(2)}) collective-permute-start(bf16[512,768]{1,0:T(8,128)(2,1)S(1)} %copy-done.3), channel_id=1, source_target_pairs={{0,2},{1,3},{2,0},{3,1},{4,6},{5,7},{6,4},{7,5},{8,10},{9,11},{10,... | collective-permute-start | bytes 2359304 | tf_op jit(solution)/shard_map/ppermute | solution.py:443
  69.2 35.0 %collective-permute-start.21 = (bf16[4,768]{1,0:T(4,128)(2,1)S(1)}, bf16[4,768]{1,0:T(4,128)(2,1)S(1)}, u32[]{:S(2)}, u32[]{:S(2)}) collective-permute-start(bf16[4,768]{1,0:T(4,128)(2,1)S(1)} %pad_maximum_fusion.18), channel_id=1, source_target_pairs={{0,2},{1,3},{2,0},{3,1},{4,6},{5,7},{6,4},{7,5},{8,10},{9,11},{10,... | collective-permute-start | bytes 18440 | tf_op jit(solution)/shard_map/ppermute | solution.py:443
  120.9 78.0 %collective-permute-start.71 = (bf16[9216,128]{1,0:T(8,128)(2,1)}, bf16[9216,128]{1,0:T(8,128)(2,1)S(1)}, u32[]{:S(2)}, u32[]{:S(2)}) collective-permute-start(bf16[9216,128]{1,0:T(8,128)(2,1)} %get-tuple-element.112), channel_id=1, source_target_pairs={{0,1},{1,0},{2,3},{3,2},{4,5},{5,4},{6,7},{7,6},{8,9},{9,8},{10,11... | collective-permute-start | bytes 7077896 | tf_op jit(solution)/shard_map/ppermute | solution.py:443
  121.7 100.6 %collective-permute-start.59 = (bf16[2304,512]{1,0:T(8,128)(2,1)}, bf16[2304,512]{1,0:T(8,128)(2,1)S(1)}, u32[]{:S(2)}, u32[]{:S(2)}) collective-permute-start(bf16[2304,512]{1,0:T(8,128)(2,1)} %get-tuple-element.108), channel_id=1, source_target_pairs={{0,1},{1,0},{2,3},{3,2},{4,5},{5,4},{6,7},{7,6},{8,9},{9,8},{10,11... | collective-permute-start | bytes 7077896 | tf_op jit(solution)/shard_map/ppermute | solution.py:443
  146.4 51.2 %collective-permute-start.18 = (bf16[512,768]{1,0:T(8,128)(2,1)}, bf16[512,768]{1,0:T(8,128)(2,1)S(1)}, u32[]{:S(2)}, u32[]{:S(2)}) collective-permute-start(bf16[512,768]{1,0:T(8,128)(2,1)} %get-tuple-element.91), channel_id=1, source_target_pairs={{0,1},{1,0},{2,3},{3,2},{4,5},{5,4},{6,7},{7,6},{8,9},{9,8},{10,11... | collective-permute-start | bytes 2359304 | tf_op jit(solution)/shard_map/ppermute | solution.py:443
  184.8 37.3 %collective-permute-start.95 = (bf16[512,768]{1,0:T(8,128)(2,1)}, bf16[512,768]{1,0:T(8,128)(2,1)S(1)}, u32[]{:S(2)}, u32[]{:S(2)}) collective-permute-start(bf16[512,768]{1,0:T(8,128)(2,1)} %get-tuple-element.126), channel_id=1, source_target_pairs={{0,8},{4,12},{8,0},{12,4},{16,24},{20,28},{24,16},{28,20},{1,9},{5... | collective-permute-start | bytes 2359304 | tf_op jit(solution)/shard_map/ppermute | solution.py:436
  200.8 38.0 %collective-permute-start.83 = (bf16[384,1024]{1,0:T(8,128)(2,1)S(1)}, bf16[384,1024]{1,0:T(8,128)(2,1)S(1)}, u32[]{:S(2)}, u32[]{:S(2)}) collective-permute-start(bf16[384,1024]{1,0:T(8,128)(2,1)S(1)} %copy-done.45), channel_id=1, source_target_pairs={{0,4},{4,0},{8,12},{12,8},{16,20},{20,16},{24,28},{28,24},{1,5},{5... | collective-permute-start | bytes 2359304 | tf_op jit(solution)/shard_map/ppermute | solution.py:436
  203.5 52.4 %collective-permute-start.86 = (bf16[384,1024]{1,0:T(8,128)(2,1)S(1)}, bf16[384,1024]{1,0:T(8,128)(2,1)S(1)}, u32[]{:S(2)}, u32[]{:S(2)}) collective-permute-start(bf16[384,1024]{1,0:T(8,128)(2,1)S(1)} %copy-done.44), channel_id=1, source_target_pairs={{0,8},{4,12},{8,0},{12,4},{16,24},{20,28},{24,16},{28,20},{1,9},{5... | collective-permute-start | bytes 2359304 | tf_op jit(solution)/shard_map/ppermute | solution.py:436
  222.3 33.7 %collective-permute-start.89 = (bf16[384,1024]{1,0:T(8,128)(2,1)S(1)}, bf16[384,1024]{1,0:T(8,128)(2,1)S(1)}, u32[]{:S(2)}, u32[]{:S(2)}) collective-permute-start(bf16[384,1024]{1,0:T(8,128)(2,1)S(1)} %copy-done.43), channel_id=1, source_target_pairs={{0,24},{4,28},{8,16},{12,20},{16,8},{20,12},{24,0},{28,4},{1,25},{... | collective-permute-start | bytes 2359304 | tf_op jit(solution)/shard_map/ppermute | solution.py:436
  222.7 68.3 %collective-permute-start.93 = (bf16[256,768]{1,0:T(8,128)(2,1)S(1)}, bf16[256,768]{1,0:T(8,128)(2,1)S(1)}, u32[]{:S(2)}, u32[]{:S(2)}) collective-permute-start(bf16[256,768]{1,0:T(8,128)(2,1)S(1)} %add_convert_fusion.6), channel_id=1, source_target_pairs={{0,8},{4,12},{8,0},{12,4},{16,24},{20,28},{24,16},{28,20},{1,9},{5... | collective-permute-start | bytes 1179656 | tf_op jit(solution)/shard_map/ppermute | solution.py:436
  239.6 49.9 %collective-permute-start.75 = (bf16[1536,128]{1,0:T(8,128)(2,1)S(1)}, bf16[1536,128]{1,0:T(8,128)(2,1)S(1)}, u32[]{:S(2)}, u32[]{:S(2)}) collective-permute-start(bf16[1536,128]{1,0:T(8,128)(2,1)S(1)} %get-tuple-element.139), channel_id=1, source_target_pairs={{0,8},{4,12},{8,0},{12,4},{16,24},{20,28},{24,16},{28,20},{1,9},{5... | collective-permute-start | bytes 1179656 | tf_op jit(solution)/shard_map/ppermute | solution.py:436
  256.0 35.8 %collective-permute-start.96 = (bf16[256,768]{1,0:T(8,128)(2,1)S(1)}, bf16[256,768]{1,0:T(8,128)(2,1)S(1)}, u32[]{:S(2)}, u32[]{:S(2)}) collective-permute-start(bf16[256,768]{1,0:T(8,128)(2,1)S(1)} %add_convert_fusion.5), channel_id=1, source_target_pairs={{0,24},{4,28},{8,16},{12,20},{16,8},{20,12},{24,0},{28,4},{1,25},{... | collective-permute-start | bytes 1179656 | tf_op jit(solution)/shard_map/ppermute | solution.py:436
  291.1 52.6 %collective-permute-start.90 = (bf16[192,1024]{1,0:T(8,128)(2,1)S(1)}, bf16[192,1024]{1,0:T(8,128)(2,1)S(1)}, u32[]{:S(2)}, u32[]{:S(2)}) collective-permute-start(bf16[192,1024]{1,0:T(8,128)(2,1)S(1)} %add_convert_fusion.7), channel_id=1, source_target_pairs={{0,4},{4,0},{8,12},{12,8},{16,20},{20,16},{24,28},{28,24},{1,5},{5... | collective-permute-start | bytes 1179656 | tf_op jit(solution)/shard_map/ppermute | solution.py:436
  316.0 82.2 %collective-permute-start.20 = (bf16[512,768]{1,0:T(8,128)(2,1)S(1)}, bf16[512,768]{1,0:T(8,128)(2,1)S(1)}, u32[]{:S(2)}, u32[]{:S(2)}) collective-permute-start(bf16[512,768]{1,0:T(8,128)(2,1)S(1)} %add_convert_fusion), channel_id=1, source_target_pairs={{0,2},{1,3},{2,0},{3,1},{4,6},{5,7},{6,4},{7,5},{8,10},{9,11},{10,... | collective-permute-start | bytes 2359304 | tf_op jit(solution)/shard_map/ppermute | solution.py:443
  316.6 52.6 %collective-permute-start.94 = (bf16[128,768]{1,0:T(8,128)(2,1)S(1)}, bf16[128,768]{1,0:T(8,128)(2,1)S(1)}, u32[]{:S(2)}, u32[]{:S(2)}) collective-permute-start(bf16[128,768]{1,0:T(8,128)(2,1)S(1)} %add_convert_fusion.24), channel_id=1, source_target_pairs={{0,24},{4,28},{8,16},{12,20},{16,8},{20,12},{24,0},{28,4},{1,25},{... | collective-permute-start | bytes 589832 | tf_op jit(solution)/shard_map/ppermute | solution.py:436
  324.3 46.6 %collective-permute-start.97 = (bf16[128,768]{1,0:T(8,128)(2,1)S(1)}, bf16[128,768]{1,0:T(8,128)(2,1)S(1)}, u32[]{:S(2)}, u32[]{:S(2)}) collective-permute-start(bf16[128,768]{1,0:T(8,128)(2,1)S(1)} %add_convert_fusion.23), channel_id=1, source_target_pairs={{0,4},{4,0},{8,12},{12,8},{16,20},{20,16},{24,28},{28,24},{1,5},{5... | collective-permute-start | bytes 589832 | tf_op jit(solution)/shard_map/ppermute | solution.py:436
  334.3 38.2 %collective-permute-start.100 = (bf16[128,768]{1,0:T(8,128)(2,1)S(1)}, bf16[128,768]{1,0:T(8,128)(2,1)S(1)}, u32[]{:S(2)}, u32[]{:S(2)}) collective-permute-start(bf16[128,768]{1,0:T(8,128)(2,1)S(1)} %add_convert_fusion.22), channel_id=1, source_target_pairs={{0,8},{4,12},{8,0},{12,4},{16,24},{20,28},{24,16},{28,20},{1,9},{5... | collective-permute-start | bytes 589832 | tf_op jit(solution)/shard_map/ppermute | solution.py:436
  384.4 41.2 %collective-permute-start.11 = (bf16[512,768]{1,0:T(8,128)(2,1)}, bf16[512,768]{1,0:T(8,128)(2,1)S(1)}, u32[]{:S(2)}, u32[]{:S(2)}) collective-permute-start(bf16[512,768]{1,0:T(8,128)(2,1)} %get-tuple-element.80), channel_id=1, source_target_pairs={{0,1},{1,0},{2,3},{3,2},{4,5},{5,4},{6,7},{7,6},{8,9},{9,8},{10,11... | collective-permute-start | bytes 2359304 | tf_op jit(solution)/shard_map/ppermute | solution.py:443
  384.4 41.2 %collective-permute-start.17 = (bf16[512,768]{1,0:T(8,128)(2,1)}, bf16[512,768]{1,0:T(8,128)(2,1)S(1)}, u32[]{:S(2)}, u32[]{:S(2)}) collective-permute-start(bf16[512,768]{1,0:T(8,128)(2,1)} %add_convert_fusion.2), channel_id=1, source_target_pairs={{0,2},{1,3},{2,0},{3,1},{4,6},{5,7},{6,4},{7,5},{8,10},{9,11},{10,... | collective-permute-start | bytes 2359304 | tf_op jit(solution)/shard_map/ppermute | solution.py:443
  392.6 43.9 %collective-permute-start.77 = (bf16[384,128]{1,0:T(8,128)(2,1)}, bf16[384,128]{1,0:T(8,128)(2,1)}, u32[]{:S(2)}, u32[]{:S(2)}) collective-permute-start(bf16[384,128]{1,0:T(8,128)(2,1)} %get-tuple-element.133), channel_id=1, source_target_pairs={{0,4},{4,0},{8,12},{12,8},{16,20},{20,16},{24,28},{28,24},{1,5},{5... | collective-permute-start | bytes 294920 | tf_op jit(solution)/shard_map/ppermute | solution.py:436
  394.5 42.5 %collective-permute-start.80 = (bf16[384,128]{1,0:T(8,128)(2,1)}, bf16[384,128]{1,0:T(8,128)(2,1)}, u32[]{:S(2)}, u32[]{:S(2)}) collective-permute-start(bf16[384,128]{1,0:T(8,128)(2,1)} %get-tuple-element.132), channel_id=1, source_target_pairs={{0,8},{4,12},{8,0},{12,4},{16,24},{20,28},{24,16},{28,20},{1,9},{5... | collective-permute-start | bytes 294920 | tf_op jit(solution)/shard_map/ppermute | solution.py:436
  398.2 41.0 %collective-permute-start.65 = (bf16[96,512]{1,0:T(8,128)(2,1)}, bf16[96,512]{1,0:T(8,128)(2,1)}, u32[]{:S(2)}, u32[]{:S(2)}) collective-permute-start(bf16[96,512]{1,0:T(8,128)(2,1)} %get-tuple-element.144), channel_id=1, source_target_pairs={{0,4},{4,0},{8,12},{12,8},{16,20},{20,16},{24,28},{28,24},{1,5},{5... | collective-permute-start | bytes 294920 | tf_op jit(solution)/shard_map/ppermute | solution.py:436
  425.7 51.0 %collective-permute-start.47 = (bf16[2304,128]{1,0:T(8,128)(2,1)}, bf16[2304,128]{1,0:T(8,128)(2,1)S(1)}, u32[]{:S(2)}, u32[]{:S(2)}) collective-permute-start(bf16[2304,128]{1,0:T(8,128)(2,1)} %get-tuple-element.105), channel_id=1, source_target_pairs={{0,1},{1,0},{2,3},{3,2},{4,5},{5,4},{6,7},{7,6},{8,9},{9,8},{10,11... | collective-permute-start | bytes 1769480 | tf_op jit(solution)/shard_map/ppermute | solution.py:443
  436.5 51.4 %collective-permute-start.35 = (bf16[2304,384]{1,0:T(8,128)(2,1)}, bf16[2304,384]{1,0:T(8,128)(2,1)}, u32[]{:S(2)}, u32[]{:S(2)}) collective-permute-start(bf16[2304,384]{1,0:T(8,128)(2,1)} %get-tuple-element.101), channel_id=1, source_target_pairs={{0,1},{1,0},{2,3},{3,2},{4,5},{5,4},{6,7},{7,6},{8,9},{9,8},{10,11... | collective-permute-start | bytes 5308424 | tf_op jit(solution)/shard_map/ppermute | solution.py:443
  (118 other events, 1774.4 us)
